TPU v7x, 512 devices: a whole 4x4x16 slice. The times are simulated.
512 devices in a mesh: dp: 8 (over z_hi, y), tm: 64 (over z_lo, x, core).
Axes of the slice: x: 4, y: 4, z: 16 (z_hi: 2, z_lo: 8; z = z_hi * 8 + z_lo), core: 2. Of those that a mesh axis runs over, the one named last changes fastest.
Arguments:
- query_proj: bfloat16 [8, 8192, 768], P('dp', 'tm'), may hold values from -240 to 240
- key_proj: bfloat16 [8, 8192, 768], P('dp', 'tm'), may hold values from -6 to 6
- value_proj: bfloat16 [8, 8192, 768], P('dp', 'tm'), may hold values from -6 to 6
- cotangent: bfloat16 [8, 8192, 768], P('dp', 'tm'), may hold values from -6 to 6
- lengths: int32 [8], P('dp'), may hold values from 4096 to 8192, as said below
- rel_bias: float32 [12, 257], replicated, may hold values from -4 to 4
Outputs:
- context: bfloat16 [8, 8192, 768], P('dp', 'tm')
- grad_query: bfloat16 [8, 8192, 768], P('dp', 'tm')
- grad_key: bfloat16 [8, 8192, 768], P('dp', 'tm')
- grad_value: bfloat16 [8, 8192, 768], P('dp', 'tm')
- grad_bias: float32 [12, 257], replicated
Inputs may be any that keep to these rules, and one draw needn't show every extreme that they name: `lengths`: one utterance has all 8192 frames valid and another exactly 4096.
All inputs are finite; a program needn't handle non-finite values.
Results may differ from a plain program's by a relative error of at most 0.005.
Values may be sent and summed in bfloat16 or wider, within the bound.
No kernel may reach another device: no remote copies, remote signals or barrier semaphores. Data moves between devices by JAX's collectives and lax.ppermute only.
A program may use at most 64 MiB of HBM per device.

v0:
```python
import jax
import jax.numpy as jnp
from jax import lax
from jax.sharding import Mesh
from jax.sharding import PartitionSpec as P

H = 12
HD = 64
W = 128
TM = ("tm_0", "tm_1", "tm_2")
DP_TM = ("dp_0", "dp_1", "tm_0", "tm_1", "tm_2")
DP = ("dp_0", "dp_1")


masked_score = -1e30


def padded_2(cells, sides, width):
    for axis, dim in sides:
        count = lax.axis_size(axis)
        ends = count - 1
        head = lax.slice_in_dim(cells, 0, width, axis=dim)
        tail = lax.slice_in_dim(cells, cells.shape[dim] - width, cells.shape[dim], axis=dim)
        cells = jnp.concatenate(
            [
                lax.ppermute(tail, axis, [(i, (i + 1) % count) for i in range(ends)]),
                cells,
                lax.ppermute(head, axis, [((i + 1) % count, i) for i in range(ends)]),
            ],
            axis=dim,
        )
    return cells


def by_axis(x, axes):
    for axis in axes:
        x = lax.psum(x, axis)
    return x


def band_matrix(bias_table, height, breadth):
    num_heads = bias_table.shape[0]
    span_cols = bias_table.shape[1]
    repeated = jnp.broadcast_to(bias_table[:, None, :], (num_heads, height, span_cols))
    padded = jnp.pad(repeated, ((0, 0), (0, 0), (0, breadth + 1 - span_cols)))
    flattened = padded.reshape(num_heads, height * (breadth + 1))[:, : height * breadth]
    return flattened.reshape(num_heads, height, breadth)


def band_sum(values, span_cols):
    num_heads, height, breadth = values.shape
    flattened = jnp.pad(values.reshape(num_heads, height * breadth), ((0, 0), (0, height)))
    return jnp.sum(flattened.reshape(num_heads, height, breadth + 1)[:, :, :span_cols], axis=1)


def heads_first(array, rows):
    return array.reshape(rows, H, HD).transpose(1, 0, 2)


def rows_first(array):
    num_heads, rows, size = array.shape
    return array.transpose(1, 0, 2).reshape(rows, num_heads * size)


def query_side(query_rows, key_rows, value_rows, grad_rows, bias_table, query_pos, key_pos, length):
    scaling = HD ** (-0.5)
    height = query_rows.shape[1]
    breadth = key_rows.shape[1]
    scores = (
        jnp.einsum("hqd,hkd->hqk", query_rows, key_rows, preferred_element_type=jnp.float32)
        * scaling
    )
    scores = scores + band_matrix(bias_table, height, breadth)
    allowed = (
        (jnp.abs(key_pos[None, :] - query_pos[:, None]) <= W)
        & (key_pos[None, :] >= 0)
        & (key_pos[None, :] < length)
    )
    scores = jnp.where(allowed[None], scores, masked_score)
    row_max = jnp.max(scores, axis=-1)
    shifted = jnp.exp(scores - row_max[..., None])
    row_total = jnp.sum(shifted, axis=-1)
    log_total = row_max + jnp.log(row_total)
    attn_probs = shifted / row_total[..., None]
    valid_rows = query_pos < length
    probs_low = attn_probs.astype(jnp.bfloat16)
    mixed = jnp.einsum("hqk,hkd->hqd", probs_low, value_rows, preferred_element_type=jnp.float32)
    context = jnp.where(valid_rows[None, :, None], mixed, 0.0).astype(jnp.bfloat16)
    masked_grad = jnp.where(valid_rows[None, :, None], grad_rows, jnp.zeros_like(grad_rows))
    grad_probs = jnp.einsum(
        "hqd,hkd->hqk", masked_grad, value_rows, preferred_element_type=jnp.float32
    )
    row_delta = jnp.sum(attn_probs * grad_probs, axis=-1)
    grad_scores = attn_probs * (grad_probs - row_delta[..., None])
    grad_low = grad_scores.astype(jnp.bfloat16)
    grad_query = (
        jnp.einsum("hqk,hkd->hqd", grad_low, key_rows, preferred_element_type=jnp.float32) * scaling
    ).astype(jnp.bfloat16)
    grad_table = band_sum(grad_scores, bias_table.shape[1])
    results = (context, grad_query, log_total, row_delta, grad_table)
    return results


def key_side(
    key_rows,
    value_rows,
    query_rows,
    grad_rows,
    log_total,
    row_delta,
    bias_table,
    key_pos,
    query_pos,
    length,
):
    scaling = HD ** (-0.5)
    height = key_rows.shape[1]
    breadth = query_rows.shape[1]
    scores = (
        jnp.einsum("hkd,hqd->hkq", key_rows, query_rows, preferred_element_type=jnp.float32)
        * scaling
    )
    scores = scores + band_matrix(bias_table[:, ::-1], height, breadth)
    valid_query = (query_pos >= 0) & (query_pos < length)
    allowed = (
        (jnp.abs(query_pos[None, :] - key_pos[:, None]) <= W)
        & (key_pos[:, None] < length)
        & valid_query[None, :]
    )
    attn_probs = jnp.where(
        allowed[None], jnp.exp(jnp.where(allowed[None], scores - log_total[:, None, :], 0.0)), 0.0
    )
    probs_low = attn_probs.astype(jnp.bfloat16)
    masked_grad = jnp.where(valid_query[None, :, None], grad_rows, jnp.zeros_like(grad_rows))
    grad_probs = jnp.einsum(
        "hkd,hqd->hkq", value_rows, masked_grad, preferred_element_type=jnp.float32
    )
    grad_scores = attn_probs * (grad_probs - row_delta[:, None, :])
    grad_low = grad_scores.astype(jnp.bfloat16)
    key_grad = (
        jnp.einsum("hkq,hqd->hkd", grad_low, query_rows, preferred_element_type=jnp.float32)
        * scaling
    )
    value_grad = jnp.einsum(
        "hkq,hqd->hkd", probs_low, masked_grad, preferred_element_type=jnp.float32
    )
    return (key_grad, value_grad)


def on_device(query_proj, key_proj, value_proj, cotangent, lengths, rel_bias):
    frames = query_proj.shape[1]
    model_width = query_proj.shape[2]
    extended = frames + 2 * W
    first_frame = lax.axis_index(TM) * frames
    query_pos = first_frame + jnp.arange(frames, dtype=jnp.int32)
    key_pos = first_frame - W + jnp.arange(extended, dtype=jnp.int32)
    length = lengths[0]
    head_group = 4
    groups = H // head_group
    with_rims = padded_2(jnp.stack([key_proj, value_proj, query_proj, cotangent]), ((TM, 2),), W)
    key_ext = heads_first(with_rims[0, 0], extended)
    value_ext = heads_first(with_rims[1, 0], extended)
    query_own = heads_first(query_proj[0], frames)
    grad_own = heads_first(cotangent[0], frames)
    outputs = []
    for group_index in range(groups):
        low_head = group_index * head_group
        high_head = low_head + head_group
        outputs.append(
            query_side(
                query_own[low_head:high_head],
                key_ext[low_head:high_head],
                value_ext[low_head:high_head],
                grad_own[low_head:high_head],
                rel_bias[low_head:high_head],
                query_pos,
                key_pos,
                length,
            )
        )
    context = rows_first(jnp.concatenate([item[0] for item in outputs], axis=0))
    grad_query = rows_first(jnp.concatenate([item[1] for item in outputs], axis=0))
    log_totals = jnp.concatenate([item[2] for item in outputs], axis=0)
    row_deltas = jnp.concatenate([item[3] for item in outputs], axis=0)
    grad_table = jnp.concatenate([item[4] for item in outputs], axis=0)
    row_stats_all = padded_2(jnp.stack([log_totals, row_deltas]), ((TM, 2),), W)
    query_ext = heads_first(with_rims[2, 0], extended)
    grad_ext = heads_first(with_rims[3, 0], extended)
    key_own = heads_first(key_proj[0], frames)
    value_own = heads_first(value_proj[0], frames)
    key_parts = []
    value_parts = []
    for group_index in range(groups):
        low_head = group_index * head_group
        high_head = low_head + head_group
        key_part, value_part = key_side(
            key_own[low_head:high_head],
            value_own[low_head:high_head],
            query_ext[low_head:high_head],
            grad_ext[low_head:high_head],
            row_stats_all[0, low_head:high_head],
            row_stats_all[1, low_head:high_head],
            rel_bias[low_head:high_head],
            query_pos,
            key_pos,
            length,
        )
        key_parts.append(key_part)
        value_parts.append(value_part)
    grad_key = rows_first(jnp.concatenate(key_parts, axis=0)).astype(jnp.bfloat16)
    grad_value = rows_first(jnp.concatenate(value_parts, axis=0)).astype(jnp.bfloat16)
    grad_bias = by_axis(grad_table, DP_TM)
    return (
        context.reshape(1, frames, model_width),
        grad_query.reshape(1, frames, model_width),
        grad_key.reshape(1, frames, model_width),
        grad_value.reshape(1, frames, model_width),
        grad_bias,
    )


def solution(mesh):
    finer = Mesh(mesh.devices.reshape(2, 4, 8, 4, 2), ("dp_0", "dp_1", "tm_0", "tm_1", "tm_2"))
    in_specs = (P(DP, TM, None), P(DP, TM, None), P(DP, TM, None), P(DP, TM, None), P(DP), P())
    out_specs = (P(DP, TM, None), P(DP, TM, None), P(DP, TM, None), P(DP, TM, None), P())
    return jax.shard_map(
        on_device, mesh=finer, in_specs=in_specs, out_specs=out_specs, check_vma=False
    )
```

profile of v0, /device:TPU:1, one launch (start us, length us, event | category | flops | bytes accessed | tf_op | source)
XLA Modules:
  0.0 190.9 jit_solution(16381931620373479713)
XLA Ops:
  0.6 1.1 copy.43
  1.7 1.1 copy.42
  2.8 1.1 copy.41
  3.9 1.2 copy.40
  5.1 1.0 pad_maximum_fusion.1
  6.1 8.7 %collective-permute-start.1 = (bf16[4,1,128,768]{2,3,1,0:T(8,128)(2,1)}, bf16[4,1,128,768]{2,3,1,0:T(8,128)(2,1)}, u32[]{:S(2)}, u32[]{:S(2)}) collective-permute-start(bf16[4,1,128,768]{2,3,1,0:T(8,128)(2,1)} %pad_maximum_fusion.1), channel_id=1, source_target_pairs={{1,0},{2,1},{3,2},{4,3},{5,4},{6,5},{7,6},{8,7},{9,8},{10,9},{11,1... | collective-permute-start | bytes 2359304 | tf_op jit(solution)/shard_map/ppermute | solution.py:28
  14.8 1.9 %collective-permute-start = (bf16[4,1,128,768]{2,3,1,0:T(8,128)(2,1)}, bf16[4,1,128,768]{2,3,1,0:T(8,128)(2,1)}, u32[]{:S(2)}, u32[]{:S(2)}) collective-permute-start(bf16[4,1,128,768]{2,3,1,0:T(8,128)(2,1)} %pad_maximum_fusion.1), channel_id=1, source_target_pairs={{0,1},{1,2},{2,3},{3,4},{4,5},{5,6},{6,7},{7,8},{8,9},{9,10},{10,1... | collective-permute-start | bytes 2359304 | tf_op jit(solution)/shard_map/ppermute | solution.py:26
  17.6 1.0 reshape.263
  19.3 1.0 reshape.261
  20.4 1.1 copy.47
  21.8 1.0 reshape.259
  22.9 1.2 copy.45
  24.6 1.0 reshape.269
  25.8 1.2 copy.67
  27.5 1.0 reshape.267
  28.7 1.2 copy.65
  30.4 1.0 reshape.265
  31.6 1.1 copy.62
  32.7 0.9 and_and_fusion
  33.6 1.6 pad_maximum_fusion
  35.2 1.3 fusion.128
  37.4 0.9 fusion.29
  38.4 0.9 fusion.28
  39.7 1.2 multiply_reduce_fusion.1
  41.4 0.9 fusion.27
  42.3 1.2 multiply_reduce_fusion.2
  44.2 3.3 %collective-permute-start.3 = (f32[2,12,128]{2,1,0:T(8,128)}, f32[2,12,128]{2,1,0:T(8,128)}, u32[]{:S(2)}, u32[]{:S(2)}) collective-permute-start(f32[2,12,128]{2,1,0:T(8,128)} %pad_maximum_fusion.7), channel_id=1, source_target_pairs={{1,0},{2,1},{3,2},{4,3},{5,4},{6,5},{7,6},{8,7},{9,8},{10,9},{11,1... | collective-permute-start | bytes 36872 | tf_op jit(solution)/shard_map/ppermute | solution.py:28
  47.5 2.4 %collective-permute-start.2 = (f32[2,12,128]{2,1,0:T(8,128)}, f32[2,12,128]{2,1,0:T(8,128)}, u32[]{:S(2)}, u32[]{:S(2)}) collective-permute-start(f32[2,12,128]{2,1,0:T(8,128)} %pad_maximum_fusion.7), channel_id=1, source_target_pairs={{0,1},{1,2},{2,3},{3,4},{4,5},{5,6},{6,7},{7,8},{8,9},{9,10},{10,1... | collective-permute-start | bytes 36872 | tf_op jit(solution)/shard_map/ppermute | solution.py:26
  50.3 1.1 copy.74
  51.5 1.3 subtract_multiply_fusion.1
  53.0 1.1 copy.73
  54.1 1.3 subtract_multiply_fusion.2
  56.0 0.8 copy.75
  56.9 0.8 copy.76
  58.4 1.0 reshape.276
  60.2 1.0 reshape.274
  62.0 1.0 reshape.272
  63.1 23.4 %psum.35 = f32[12,257]{1,0:T(8,128)S(1)} all-reduce(f32[12,257]{1,0:T(8,128)S(1)} %pad_maximum_fusion.6), channel_id=1, replica_groups=mesh['dp_0'=2,'dp_1'=4,'tm_0'=8,'tm_1'=4,'tm_2'=2] {'dp_0'}, use_global_device_ids=true, to_apply=%region_12.13 | all-reduce | flops 3084 | bytes 24672 | tf_op jit(solution)/shard_map/psum | solution.py:37
  86.5 13.5 %psum.36 = f32[12,257]{1,0:T(8,128)S(1)} all-reduce(f32[12,257]{1,0:T(8,128)S(1)} %psum.35), channel_id=1, replica_groups=mesh['dp_0'=2,'dp_1'=4,'tm_0'=8,'tm_1'=4,'tm_2'=2] {'dp_1'}, use_global_device_ids=true, to_apply=%region_13.14 | all-reduce | flops 3084 | bytes 24672 | tf_op jit(solution)/shard_map/psum | solution.py:37
  100.0 45.1 %psum.37 = f32[12,257]{1,0:T(8,128)S(1)} all-reduce(f32[12,257]{1,0:T(8,128)S(1)} %psum.36), channel_id=1, replica_groups=mesh['dp_0'=2,'dp_1'=4,'tm_0'=8,'tm_1'=4,'tm_2'=2] {'tm_0'}, use_global_device_ids=true, to_apply=%region_14.15 | all-reduce | flops 3084 | bytes 24672 | tf_op jit(solution)/shard_map/psum | solution.py:37
  145.1 15.4 %psum.38 = f32[12,257]{1,0:T(8,128)S(1)} all-reduce(f32[12,257]{1,0:T(8,128)S(1)} %psum.37), channel_id=1, replica_groups=mesh['dp_0'=2,'dp_1'=4,'tm_0'=8,'tm_1'=4,'tm_2'=2] {'tm_1'}, use_global_device_ids=true, to_apply=%region_15.16 | all-reduce | flops 3084 | bytes 24672 | tf_op jit(solution)/shard_map/psum | solution.py:37
  160.5 19.3 %psum.39 = f32[12,257]{1,0:T(8,128)} all-reduce(f32[12,257]{1,0:T(8,128)S(1)} %psum.38), channel_id=1, replica_groups=mesh['dp_0'=2,'dp_1'=4,'tm_0'=8,'tm_1'=4,'tm_2'=2] {'tm_2'}, use_global_device_ids=true, to_apply=%region_16.17 | all-reduce | flops 3084 | bytes 24672 | tf_op jit(solution)/shard_map/psum | solution.py:37
  179.8 0.8 maximum_bitcast_fusion.5
  180.6 1.6 fusion.5
  184.6 1.7 fusion.35
  186.3 1.7 fusion.34
  189.2 0.8 copy.77
  190.1 0.8 copy.78
  (121 shorter events, 12.3 us)
Async XLA Ops:
  0.6 16.1 %copy-start.20 = (f32[12,257]{1,0:T(8,128)S(1)}, f32[12,257]{1,0:T(8,128)}, u32[]{:S(2)}) copy-start(f32[12,257]{1,0:T(8,128)} %param.11) | copy-start | bytes 37012
  3.9 29.7 %copy-start.5 = (bf16[1,128,768]{1,2,0:T(8,128)(2,1)}, bf16[1,128,768]{1,2,0:T(8,128)(2,1)S(1)}, u32[]{:S(2)}) copy-start(bf16[1,128,768]{1,2,0:T(8,128)(2,1)S(1)} %copy.41) | copy-start | bytes 589828
  5.1 28.5 %copy-start.7 = (bf16[1,128,768]{1,2,0:T(8,128)(2,1)}, bf16[1,128,768]{1,2,0:T(8,128)(2,1)S(1)}, u32[]{:S(2)}) copy-start(bf16[1,128,768]{1,2,0:T(8,128)(2,1)S(1)} %copy.40) | copy-start | bytes 589828
  6.1 27.5 %collective-permute-start.1 = (bf16[4,1,128,768]{2,3,1,0:T(8,128)(2,1)}, bf16[4,1,128,768]{2,3,1,0:T(8,128)(2,1)}, u32[]{:S(2)}, u32[]{:S(2)}) collective-permute-start(bf16[4,1,128,768]{2,3,1,0:T(8,128)(2,1)} %pad_maximum_fusion.1), channel_id=1, source_target_pairs={{1,0},{2,1},{3,2},{4,3},{5,4},{6,5},{7,6},{8,7},{9,8},{10,9},{11,1... | collective-permute-start | bytes 2359304 | tf_op jit(solution)/shard_map/ppermute | solution.py:28
  14.8 18.8 %collective-permute-start = (bf16[4,1,128,768]{2,3,1,0:T(8,128)(2,1)}, bf16[4,1,128,768]{2,3,1,0:T(8,128)(2,1)}, u32[]{:S(2)}, u32[]{:S(2)}) collective-permute-start(bf16[4,1,128,768]{2,3,1,0:T(8,128)(2,1)} %pad_maximum_fusion.1), channel_id=1, source_target_pairs={{0,1},{1,2},{2,3},{3,4},{4,5},{5,6},{6,7},{7,8},{8,9},{9,10},{10,1... | collective-permute-start | bytes 2359304 | tf_op jit(solution)/shard_map/ppermute | solution.py:26
  35.2 1.7 copy-start.1
  39.7 1.2 copy-start
  43.6 6.4 %copy-start.14 = (f32[1,12,128]{2,1,0:T(8,128)}, f32[1,12,128]{2,1,0:T(8,128)S(1)}, u32[]{:S(2)}) copy-start(f32[1,12,128]{2,1,0:T(8,128)S(1)} %maximum_bitcast_fusion) | copy-start | bytes 18436
  44.2 135.6 %collective-permute-start.3 = (f32[2,12,128]{2,1,0:T(8,128)}, f32[2,12,128]{2,1,0:T(8,128)}, u32[]{:S(2)}, u32[]{:S(2)}) collective-permute-start(f32[2,12,128]{2,1,0:T(8,128)} %pad_maximum_fusion.7), channel_id=1, source_target_pairs={{1,0},{2,1},{3,2},{4,3},{5,4},{6,5},{7,6},{8,7},{9,8},{10,9},{11,1... | collective-permute-start | bytes 36872 | tf_op jit(solution)/shard_map/ppermute | solution.py:28
  47.5 132.3 %collective-permute-start.2 = (f32[2,12,128]{2,1,0:T(8,128)}, f32[2,12,128]{2,1,0:T(8,128)}, u32[]{:S(2)}, u32[]{:S(2)}) collective-permute-start(f32[2,12,128]{2,1,0:T(8,128)} %pad_maximum_fusion.7), channel_id=1, source_target_pairs={{0,1},{1,2},{2,3},{3,4},{4,5},{5,6},{6,7},{7,8},{8,9},{9,10},{10,1... | collective-permute-start | bytes 36872 | tf_op jit(solution)/shard_map/ppermute | solution.py:26
  54.1 1.9 copy-start.16
  54.1 1.9 copy-start.17
  54.1 1.9 copy-start.18
  55.5 2.2 %copy-start.2 = (f32[4,128,384]{2,1,0:T(8,128)S(1)}, f32[4,128,384]{2,1,0:T(8,128)}, u32[]{:S(2)}) copy-start(f32[4,128,384]{2,1,0:T(8,128)} %copy.74) | copy-start | bytes 2359300
  58.2 1.3 copy-start.3
  61.8 118.0 %copy-start.15 = (f32[1,12,128]{2,1,0:T(8,128)S(1)}, f32[1,12,128]{2,1,0:T(8,128)}, u32[]{:S(2)}) copy-start(f32[1,12,128]{2,1,0:T(8,128)} %copy-done.14) | copy-start | bytes 18436
  61.8 118.8 %copy-start.8 = (bf16[1,128,768]{1,2,0:T(8,128)(2,1)S(1)}, bf16[1,128,768]{1,2,0:T(8,128)(2,1)}, u32[]{:S(2)}) copy-start(bf16[1,128,768]{1,2,0:T(8,128)(2,1)} %copy-done.7) | copy-start | bytes 589828
  61.8 118.8 %copy-start.13 = (bf16[1,1,384,768]{2,3,1,0:T(8,128)(2,1)S(1)}, bf16[1,1,384,768]{2,3,1,0:T(8,128)(2,1)}, u32[]{:S(2)}) copy-start(bf16[1,1,384,768]{2,3,1,0:T(8,128)(2,1)} %get-tuple-element.18) | copy-start | bytes 1769476
  61.8 118.8 %copy-start.19 = (pred[128,384]{0,1:T(8,128)(4,1)S(1)}, pred[128,384]{0,1:T(8,128)(4,1)}, u32[]{:S(2)}) copy-start(pred[128,384]{0,1:T(8,128)(4,1)} %get-tuple-element.30) | copy-start | bytes 147460
  62.0 120.3 %copy-start.10 = (f32[4,128,384]{1,2,0:T(8,128)S(1)}, f32[4,128,384]{1,2,0:T(8,128)}, u32[]{:S(2)}) copy-start(f32[4,128,384]{1,2,0:T(8,128)} %copy.65) | copy-start | bytes 2359300
  180.6 2.2 %copy-start.4 = (bf16[1,1,384,768]{2,3,1,0:T(8,128)(2,1)S(1)}, bf16[1,1,384,768]{2,3,1,0:T(8,128)(2,1)}, u32[]{:S(2)}) copy-start(bf16[1,1,384,768]{2,3,1,0:T(8,128)(2,1)} %get-tuple-element.17) | copy-start | bytes 1769476
  182.3 1.6 copy-start.12
  182.3 2.3 %copy-start.6 = (bf16[1,128,768]{1,2,0:T(8,128)(2,1)S(1)}, bf16[1,128,768]{1,2,0:T(8,128)(2,1)}, u32[]{:S(2)}) copy-start(bf16[1,128,768]{1,2,0:T(8,128)(2,1)} %copy-done.5) | copy-start | bytes 589828
  182.8 0.9 copy-start.11
  182.8 5.2 %copy-start.9 = (f32[4,128,384]{1,2,0:T(8,128)S(1)}, f32[4,128,384]{1,2,0:T(8,128)}, u32[]{:S(2)}) copy-start(f32[4,128,384]{1,2,0:T(8,128)} %copy.62) | copy-start | bytes 2359300
where the time goes:
time: 192 us; the launch traced here: 191 us
  blocking collectives  117 us (61%)
  local copies, waits for them, and re-layouts  32.3 us (17%)
  starting transfers between devices  16.4 us (9%)
  matrix products  14.2 us (7%)
  other arithmetic  9.12 us (5%)
  between operations  2.11 us (1%)
    psum x5, blocking collectives, by_axis(): x = lax.psum(x, axis)  117 us
    ppermute x2, starting transfers between devices, padded_2(): lax.ppermute(head, axis, [((i + 1) % count, i) for i in range(ends)])  12 us
    unnamed x65, local copies, waits for them, and re-layouts  11.4 us
    reshape x6, local copies, waits for them, and re-layouts, band_matrix(): padded.reshape(num_heads, height * (breadth + 1))[:, :height * breadth]  6.24 us
    reshape x6, local copies, waits for them, and re-layouts, band_matrix(): return flattened.reshape(num_heads, height, breadth)  6.05 us
    ppermute x2, starting transfers between devices, padded_2(): lax.ppermute(tail, axis, [(i, (i + 1) % count) for i in range(ends)])  4.34 us
    dot_general x3, matrix products, key_side(): jnp.einsum('hkq,hqd->hkd', grad_low, query_rows, preferred_element_type=j...  3.87 us
  transfers between devices with their start and end apart: 4, of which 0 were waited for; matrix products, arithmetic and copies ran while one was open for 15% of the time, Pallas kernels for 0%

commit v1 on v0

v1 whole, which is shorter than its diff:
```python
import functools

import jax
import jax.numpy as jnp
from jax import lax
from jax.experimental import pallas as pl
from jax.experimental.pallas import tpu as pltpu
from jax.sharding import Mesh
from jax.sharding import PartitionSpec as P

H = 12
HD = 64
W = 128
F = 128
D = 768
PAIRS = 6
AXES = ("dp_0", "dp_1", "tm_0", "tm_1", "tm_2")
TM = ("tm_0", "tm_1", "tm_2")
DP = ("dp_0", "dp_1")
Z16 = ("dp_0", "tm_0")
X8 = ("tm_1", "tm_2")
Y4 = ("dp_1",)
NEG = -1e30
ROWS = 32
f32 = jnp.float32
bf16 = jnp.bfloat16

NT = (((1,), (1,)), ((), ()))
NN = (((1,), (0,)), ((), ()))


def dot(a, b, dims=NN):
    return lax.dot_general(a, b, dims, preferred_element_type=f32)


def attention_kernel(
    info, q_ref, g_ref, k_ref, v_ref, left_ref, right_ref, rt_ref, t0_ref,
    ctx_ref, dq_ref, dk_ref, dv_ref, dl_ref, dr_ref, gb_ref, acc_ref, diag_ref,
):
    pair = pl.program_id(0)
    first, length = info[0], info[1]
    row = lax.broadcasted_iota(jnp.int32, (F, F), 0)
    lane = lax.broadcasted_iota(jnp.int32, (F, F), 1)
    low = lane < HD
    valid = (first + row) < length
    zero = jnp.zeros((F, F), bf16)

    q = q_ref[...] * jnp.asarray(HD**-0.5, bf16)
    g = jnp.where(valid, g_ref[...], zero)
    q2 = jnp.concatenate([jnp.where(low, q, zero), jnp.where(low, zero, q)], axis=0)
    g2 = jnp.concatenate([jnp.where(low, g, zero), jnp.where(low, zero, g)], axis=0)
    keys = (left_ref[0], k_ref[...], right_ref[0])
    values = (left_ref[1], v_ref[...], right_ref[1])

    below = lane < row
    on = lane == row
    biases = ([], [], [])
    for h in range(2):
        head = 2 * pair + h
        u0 = pltpu.roll(jnp.broadcast_to(rt_ref[2 * head], (F, F)), 0, 1, stride=1, stride_axis=0)
        u1 = pltpu.roll(jnp.broadcast_to(rt_ref[2 * head + 1], (F, F)), 0, 1, stride=1, stride_axis=0)
        biases[0].append(jnp.where(below, u0, jnp.where(on, jnp.broadcast_to(t0_ref[head], (F, F)), NEG)))
        biases[1].append(jnp.where(below, u1, u0))
        biases[2].append(jnp.where(below, NEG, u1))

    scores = []
    for a in range(3):
        pos = first + (a - 1) * W + lax.broadcasted_iota(jnp.int32, (F, 2 * F), 0)
        s = dot(keys[a], q2, NT) + jnp.concatenate(biases[a], axis=1)
        scores.append(jnp.where((pos >= 0) & (pos < length), s, NEG))
    top = functools.reduce(jnp.maximum, [jnp.max(s, axis=0, keepdims=True) for s in scores])
    exps = [jnp.exp(s - top) for s in scores]
    total = functools.reduce(jnp.add, [jnp.sum(e, axis=0, keepdims=True) for e in exps])
    inverse = 1.0 / total
    probs = [e * inverse for e in exps]
    gp = [dot(v, g2, NT) for v in values]
    delta = functools.reduce(jnp.add, [jnp.sum(p * d, axis=0, keepdims=True) for p, d in zip(probs, gp)])
    ds = [p * (d - delta) for p, d in zip(probs, gp)]
    p_low = [p.astype(bf16) for p in probs]
    ds_low = [d.astype(bf16) for d in ds]

    ctx_t = sum(dot(jnp.transpose(v), p) for v, p in zip(values, p_low))
    dq_t = sum(dot(jnp.transpose(k), d) for k, d in zip(keys, ds_low))
    ctx = jnp.transpose(jnp.concatenate([ctx_t[:HD, :F], ctx_t[HD:, F:]], axis=0))
    ctx_ref[...] = jnp.where(valid, ctx, 0.0).astype(bf16)
    dq = jnp.transpose(jnp.concatenate([dq_t[:HD, :F], dq_t[HD:, F:]], axis=0))
    dq_ref[...] = (dq * (HD**-0.5)).astype(bf16)

    dk_ref[...] = dot(ds_low[1], q2)
    dv_ref[...] = dot(p_low[1], g2)
    dl_ref[0] = dot(ds_low[0], q2).astype(bf16)
    dl_ref[1] = dot(p_low[0], g2).astype(bf16)
    dr_ref[0] = dot(ds_low[2], q2).astype(bf16)
    dr_ref[1] = dot(p_low[2], g2).astype(bf16)

    for h in range(2):
        part = [d[:, h * F : (h + 1) * F] for d in ds]
        y1 = jnp.where(below, part[0], part[1])
        y2 = jnp.where(below, part[1], part[2])
        y3 = jnp.where(on, part[0], 0.0)
        for y, ref, at in ((y1, acc_ref, 2 * pair + h), (y2, acc_ref, H + 2 * pair + h)):
            total_y = y[:8]
            for k in range(1, 16):
                total_y = total_y + pltpu.roll(y[8 * k : 8 * k + 8], F - 8 * k, 1)
            ref[at] = total_y
        diag_ref[2 * pair + h] = jnp.sum(y3, axis=0, keepdims=True)

    @pl.when(pair == PAIRS - 1)
    def _():
        summed = acc_ref[:, 0, :]
        for s in range(1, 8):
            summed = summed + pltpu.roll(acc_ref[:, s, :], F - s, 1)
        l0 = lax.broadcasted_iota(jnp.int32, (F, F), 0)
        flip = jnp.where((l0 + lane == F) | ((l0 == 0) & (lane == 0)), 1.0, 0.0).astype(f32)
        turned = lax.dot_general(summed, flip, NN, precision=lax.Precision.HIGHEST, preferred_element_type=f32)
        at0 = lax.broadcasted_iota(jnp.int32, (H, F), 1) == 0
        zed = jnp.sum(diag_ref[:, 0, :], axis=1, keepdims=True)
        one, two = turned[:H], turned[H:]
        gb_ref[:H] = jnp.where(at0, zed, one)
        gb_ref[H : 2 * H] = jnp.where(at0, one[:, :1], two)
        spot = lax.broadcasted_iota(jnp.int32, (H, F), 0) == lax.broadcasted_iota(jnp.int32, (H, F), 1)
        last = jnp.sum(jnp.where(spot, two[:, :1], 0.0), axis=0, keepdims=True)
        gb_ref[2 * H :] = jnp.broadcast_to(last, (ROWS - 2 * H, F))


def attention(info, q, g, k, v, left, right, rt, t0):
    tile = pl.BlockSpec((F, F), lambda p, *_: (0, p))
    both = pl.BlockSpec((2, F, F), lambda p, *_: (0, 0, p))
    whole = lambda shape: pl.BlockSpec(shape, lambda p, *_: (0,) * len(shape))
    return pl.pallas_call(
        attention_kernel,
        grid_spec=pltpu.PrefetchScalarGridSpec(
            num_scalar_prefetch=1,
            grid=(PAIRS,),
            in_specs=[tile, tile, tile, tile, both, both, whole((2 * H, 1, F)), whole((H, 1, F))],
            out_specs=[tile, tile, tile, tile, both, both, whole((ROWS, F))],
            scratch_shapes=[pltpu.VMEM((2 * H, 8, F), f32), pltpu.VMEM((H, 1, F), f32)],
        ),
        out_shape=[
            jax.ShapeDtypeStruct((F, D), bf16),
            jax.ShapeDtypeStruct((F, D), bf16),
            jax.ShapeDtypeStruct((F, D), f32),
            jax.ShapeDtypeStruct((F, D), f32),
            jax.ShapeDtypeStruct((2, F, D), bf16),
            jax.ShapeDtypeStruct((2, F, D), bf16),
            jax.ShapeDtypeStruct((ROWS, F), f32),
        ],
        name="attention",
    )(info, q, g, k, v, left, right, rt, t0)


def assemble_kernel(z_ref, out_ref):
    total = jnp.sum(z_ref[...].astype(f32), axis=0)
    out_ref[:, :F] = total[:H]
    out_ref[:, F : 2 * F] = total[H : 2 * H]
    spot = lax.broadcasted_iota(jnp.int32, (H, F), 0) == lax.broadcasted_iota(jnp.int32, (H, F), 1)
    out_ref[:, 2 * F :] = jnp.sum(jnp.where(spot, total[2 * H : 2 * H + 1], 0.0), axis=1, keepdims=True)


def assemble(z):
    return pl.pallas_call(
        assemble_kernel, out_shape=jax.ShapeDtypeStruct((H, 2 * W + 1), f32), name="assemble"
    )(z)


def exchange(y, axes, dtype):
    count = 1
    for axis in axes:
        count *= lax.axis_size(axis)
    sent = jnp.broadcast_to(y.astype(dtype)[None], (count,) + y.shape)
    return lax.all_to_all(sent, axes, 0, 0, tiled=True)


def on_device(query_proj, key_proj, value_proj, cotangent, lengths, rel_bias):
    first = lax.axis_index(TM) * F
    info = jnp.stack([first.astype(jnp.int32), lengths[0]])
    ends = lax.axis_size(TM) - 1
    ahead = [(i, i + 1) for i in range(ends)]
    back = [(i + 1, i) for i in range(ends)]
    kv = jnp.concatenate([key_proj, value_proj], axis=0)
    left = lax.ppermute(kv, TM, ahead)
    right = lax.ppermute(kv, TM, back)
    rt = rel_bias[:, :0:-1].reshape(H, 2, F)[:, ::-1].reshape(2 * H, 1, F)
    t0 = jnp.broadcast_to(rel_bias[:, :1, None], (H, 1, F))
    ctx, dq, dk, dv, dl, dr, gb = attention(
        info, query_proj[0], cotangent[0], key_proj[0], value_proj[0], left, right, rt, t0
    )
    from_right = lax.ppermute(dl, TM, back)
    from_left = lax.ppermute(dr, TM, ahead)
    z = exchange(gb, Z16, bf16)
    z = exchange(jnp.sum(z.astype(f32), axis=0), X8, f32)
    z = exchange(jnp.sum(z, axis=0), Y4, f32)
    grad_bias = assemble(z)
    both = from_right.astype(f32) + from_left.astype(f32)
    grad_key = (dk + both[0]).astype(bf16)
    grad_value = (dv + both[1]).astype(bf16)
    return ctx[None], dq[None], grad_key[None], grad_value[None], grad_bias


def solution(mesh):
    finer = Mesh(mesh.devices.reshape(2, 4, 8, 4, 2), AXES)
    in_specs = (P(DP, TM, None), P(DP, TM, None), P(DP, TM, None), P(DP, TM, None), P(DP), P())
    out_specs = (P(DP, TM, None), P(DP, TM, None), P(DP, TM, None), P(DP, TM, None), P())
    return jax.shard_map(
        on_device, mesh=finer, in_specs=in_specs, out_specs=out_specs, check_vma=False
    )
```

time: 192 us -> 78.9 us (0.41)
  blocking collectives: 117 us -> 0 us
  starting transfers between devices: 16.4 us -> 45.7 us
  local copies, waits for them, and re-layouts: 32.3 us -> 5.37 us
  matrix products: 14.2 us -> 0 us
  waiting for transfers between devices: 0.01 us -> 13.4 us
  Pallas kernels: 0 us -> 9.61 us
  other arithmetic: 9.12 us -> 2.32 us
    psum x5 -> x0, blocking collectives: 117 us -> none  [by_axis(): x = lax.psum(x, axis)]
    all_to_all x0 -> x3, starting transfers between devices: none -> 25.2 us  [exchange(): return lax.all_to_all(sent, axes, 0, 0, tiled=True)]
    reshape x15 -> x1, local copies, waits for them, and re-layouts: 15.3 us -> 0.01 us  [on_device(): rt = rel_bias[:, :0:-1].reshape(H, 2, F)[:, ::-1].reshape(2 * H, 1, F)]
    dot_general x21 -> x0, matrix products: 14.2 us -> none  [the longest x3 3.87 us: key_side(): jnp.einsum('hkq,hqd->hkd', grad_low, query_rows, preferred_element_type=j...]
    all_to_all x0 -> x3, waiting for transfers between devices: none -> 10.9 us  [exchange(): return lax.all_to_all(sent, axes, 0, 0, tiled=True)]
    unnamed x65 -> x17, local copies, waits for them, and re-layouts: 11.4 us -> 1.68 us
    pallas_call x0 -> x2, Pallas kernels: none -> 9.61 us  [the longest x1 8.08 us: attention(): pl.pallas_call(attention_kernel, grid_spec=pltpu.PrefetchScalarGridSpec(n...]
    ppermute x4, starting transfers between devices: 16.4 us -> 20.5 us  [the longest x1 8.75 us: on_device(): right = lax.ppermute(kv, TM, back)]
  transfers between devices with their start and end apart: 4 -> 7, of which waited for: 0 -> 4; matrix products, arithmetic and copies ran while one was open for 15% -> 4% of each run, Pallas kernels for 0% -> 0%
where the time goes in v1:
time: 78.9 us; the launch traced here: 77.8 us
  starting transfers between devices  45.7 us (58%)
  waiting for transfers between devices  13.4 us (17%)
  Pallas kernels  9.61 us (12%)
  local copies, waits for them, and re-layouts  5.37 us (7%)
  other arithmetic  2.32 us (3%)
  between operations  1.42 us (2%)
    all_to_all x3, starting transfers between devices, exchange(): return lax.all_to_all(sent, axes, 0, 0, tiled=True)  25.2 us
    all_to_all x3, waiting for transfers between devices, exchange(): return lax.all_to_all(sent, axes, 0, 0, tiled=True)  10.9 us
    ppermute x1, starting transfers between devices, on_device(): right = lax.ppermute(kv, TM, back)  8.75 us
    pallas_call x1, Pallas kernels, attention(): pl.pallas_call(attention_kernel, grid_spec=pltpu.PrefetchScalarGridSpec(n...  8.08 us
    ppermute x1, starting transfers between devices, on_device(): from_right = lax.ppermute(dl, TM, back)  7.87 us
    ppermute x1, waiting for transfers between devices, on_device(): left = lax.ppermute(kv, TM, ahead)  2.42 us
    broadcast_in_dim x3, local copies, waits for them, and re-layouts, exchange(): sent = jnp.broadcast_to(y.astype(dtype)[None], (count,) + y.shape)  1.98 us
    ppermute x1, starting transfers between devices, on_device(): left = lax.ppermute(kv, TM, ahead)  1.92 us
  transfers between devices with their start and end apart: 7, of which 4 were waited for; matrix products, arithmetic and copies ran while one was open for 4% of the time, Pallas kernels for 0%

profile of v1, /device:TPU:1, one launch (start us, length us, event | category | flops | bytes accessed | tf_op | source)
XLA Modules:
  0.0 77.8 jit_solution(6805355979275001050)
XLA Ops:
  0.6 0.0 copy-start
  0.6 1.0 %constant_dynamic-update-slice_fusion.1 = bf16[2,128,768]{2,1,0:T(8,128)(2,1)S(1)} fusion(bf16[1,128,768]{2,1,0:T(8,128)(2,1)} %param.7), kind=kLoop, calls=%fused_computation.12 | loop fusion | bytes 393216
  1.6 0.0 copy-done
  1.7 0.0 copy-start.6
  1.7 8.7 %collective-permute-start.1 = (bf16[2,128,768]{2,1,0:T(8,128)(2,1)S(1)}, bf16[2,128,768]{2,1,0:T(8,128)(2,1)S(1)}, u32[]{:S(2)}, u32[]{:S(2)}) collective-permute-start(bf16[2,128,768]{2,1,0:T(8,128)(2,1)S(1)} %constant_dynamic-update-slice_fusion), channel_id=1, source_target_pairs={{1,0},{2,1},{3,2},{4,3},{5,4},{6,5},{7,6},{8,7},{9,8},{10,9},{11,1... | collective-permute-start | bytes 1179656 | tf_op jit(solution)/shard_map/ppermute | solution.py:182
  10.4 1.9 %collective-permute-start = (bf16[2,128,768]{2,1,0:T(8,128)(2,1)S(1)}, bf16[2,128,768]{2,1,0:T(8,128)(2,1)S(1)}, u32[]{:S(2)}, u32[]{:S(2)}) collective-permute-start(bf16[2,128,768]{2,1,0:T(8,128)(2,1)S(1)} %constant_dynamic-update-slice_fusion), channel_id=1, source_target_pairs={{0,1},{1,2},{2,3},{3,4},{4,5},{5,6},{6,7},{7,8},{8,9},{9,10},{10,1... | collective-permute-start | bytes 1179656 | tf_op jit(solution)/shard_map/ppermute | solution.py:181
  13.0 0.0 copy-done.6
  13.0 0.1 slice.12
  13.1 0.1 rev.6
  13.3 0.6 rev.7
  13.9 0.6 pad_add_fusion.info
  14.5 0.1 slice_reduce_fusion
  14.6 0.0 collective-permute-done.1.right_ref
  14.6 0.0 copy-start.1
  14.6 2.4 %collective-permute-done.left_ref = bf16[2,128,768]{2,1,0:T(8,128)(2,1)S(1)} collective-permute-done((bf16[2,128,768]{2,1,0:T(8,128)(2,1)S(1)}, bf16[2,128,768]{2,1,0:T(8,128)(2,1)S(1)}, u32[]{:S(2)}, u32[]{:S(2)}) %collective-permute-start) | collective-permute-done | bytes 393248 | tf_op jit(solution)/shard_map/ppermute | solution.py:181
  17.1 0.0 copy-start.2
  17.1 0.7 broadcast_in_dim.19.t0_ref
  17.8 0.0 copy-done.1
  17.8 0.0 copy-done.2
  17.8 8.1 %attention.1 = (bf16[128,768]{1,0:T(8,128)(2,1)}, bf16[128,768]{1,0:T(8,128)(2,1)}, f32[128,768]{1,0:T(8,128)}, f32[128,768]{1,0:T(8,128)}, bf16[2,128,768]{2,1,...) custom-call(s32[2]{0:T(128)} %pad_add_fusion.info, bf16[128,768]{1,0:T(8,128)(2,1)} %bitcast.30, ...), custom_call_target="tpu_custom_call" | custom-call | tf_op jit(solution)/shard_map/attention/pallas_call | solution.py:130
  25.9 0.0 copy-start.7
  25.9 0.8 convert_element_type.22
  26.7 0.7 broadcast_in_dim.44
  27.4 10.7 %all-to-all-start = ((bf16[16,32,128]{2,1,0:T(8,128)(2,1)}), bf16[16,32,128]{2,1,0:T(8,128)(2,1)S(1)}, u32[]{:S(2)}, u32[]{:S(2)}) async-start(bf16[16,32,128]{2,1,0:T(8,128)(2,1)} %broadcast_in_dim.44), calls=%async_computation | async-start | bytes 262144 | tf_op jit(solution)/shard_map/all_to_all | solution.py:171
  38.0 7.9 %collective-permute-start.2 = (bf16[2,128,768]{2,1,0:T(8,128)(2,1)}, bf16[2,128,768]{2,1,0:T(8,128)(2,1)S(1)}, u32[]{:S(2)}, u32[]{:S(2)}) collective-permute-start(bf16[2,128,768]{2,1,0:T(8,128)(2,1)} %get-tuple-element.15), channel_id=1, source_target_pairs={{1,0},{2,1},{3,2},{4,3},{5,4},{6,5},{7,6},{8,7},{9,8},{10,9},{11,1... | collective-permute-start | bytes 1179656 | tf_op jit(solution)/shard_map/ppermute | solution.py:188
  45.9 0.0 copy-done.7
  45.9 1.9 %collective-permute-start.3 = (bf16[2,128,768]{2,1,0:T(8,128)(2,1)S(1)}, bf16[2,128,768]{2,1,0:T(8,128)(2,1)S(1)}, u32[]{:S(2)}, u32[]{:S(2)}) collective-permute-start(bf16[2,128,768]{2,1,0:T(8,128)(2,1)S(1)} %copy-done.7), channel_id=1, source_target_pairs={{0,1},{1,2},{2,3},{3,4},{4,5},{5,6},{6,7},{7,8},{8,9},{9,10},{10,1... | collective-permute-start | bytes 1179656 | tf_op jit(solution)/shard_map/ppermute | solution.py:189
  47.8 2.1 %all-to-all-done = bf16[16,32,128]{2,1,0:T(8,128)(2,1)S(1)} async-done(((bf16[16,32,128]{2,1,0:T(8,128)(2,1)}), bf16[16,32,128]{2,1,0:T(8,128)(2,1)S(1)}, u32[]{:S(2)}, u32[]{:S(2)}) %all-to-all-start) | async-done | bytes 131104 | tf_op jit(solution)/shard_map/all_to_all | solution.py:171
  50.0 0.7 broadcast_in_dim.45
  50.7 10.4 %all-to-all-start.1 = ((f32[8,32,128]{2,1,0:T(8,128)}), f32[8,32,128]{2,1,0:T(8,128)S(1)}, u32[]{:S(2)}, u32[]{:S(2)}) async-start(f32[8,32,128]{2,1,0:T(8,128)} %broadcast_in_dim.45), calls=%async_computation.1 | async-start | bytes 262144 | tf_op jit(solution)/shard_map/all_to_all | solution.py:171
  61.0 0.0 collective-permute-done.2
  61.0 0.0 collective-permute-done.3
  61.1 0.0 copy-start.3
  61.1 0.0 copy-start.4
  61.1 0.1 convert_add_fusion
  61.2 5.1 %all-to-all-done.1 = f32[8,32,128]{2,1,0:T(8,128)S(1)} async-done(((f32[8,32,128]{2,1,0:T(8,128)}), f32[8,32,128]{2,1,0:T(8,128)S(1)}, u32[]{:S(2)}, u32[]{:S(2)}) %all-to-all-start.1) | async-done | bytes 131104 | tf_op jit(solution)/shard_map/all_to_all | solution.py:171
  66.3 0.6 broadcast_in_dim.46
  67.0 4.2 %all-to-all-start.2 = ((f32[4,32,128]{2,1,0:T(8,128)}), f32[4,32,128]{2,1,0:T(8,128)S(1)}, u32[]{:S(2)}, u32[]{:S(2)}) async-start(f32[4,32,128]{2,1,0:T(8,128)} %broadcast_in_dim.46), calls=%async_computation.2 | async-start | bytes 131072 | tf_op jit(solution)/shard_map/all_to_all | solution.py:171
  71.1 0.0 copy-done.3
  71.1 0.0 copy-done.4
  71.2 0.8 %fusion.5 = (bf16[1,128,768]{2,1,0:T(8,128)(2,1)}, bf16[1,128,768]{2,1,0:T(8,128)(2,1)}) fusion(f32[128,768]{1,0:T(8,128)S(1)} %copy-done.4, f32[2,128,768]{2,1,0:T(8,128)S(1)} %convert_add_fusion, f32[128,768]{1,0:T(8,128)S(1)} %copy-done.3), kind=kLoop, calls=%fused_computation.9 | loop fusion | flops 393216 | bytes 1966080 | tf_op jit(solution)/shard_map/broadcast_in_dim | solution.py:197
  72.0 3.7 %all-to-all-done.2.z_ref = f32[4,32,128]{2,1,0:T(8,128)S(1)} async-done(((f32[4,32,128]{2,1,0:T(8,128)}), f32[4,32,128]{2,1,0:T(8,128)S(1)}, u32[]{:S(2)}, u32[]{:S(2)}) %all-to-all-start.2) | async-done | bytes 65568 | tf_op jit(solution)/shard_map/all_to_all | solution.py:171
  75.6 0.0 copy-start.5
  75.6 0.6 copy-done.5
  76.2 1.5 %assemble.1 = f32[12,257]{1,0:T(8,128)} custom-call(f32[4,32,128]{2,1,0:T(8,128)} %copy-done.5), custom_call_target="tpu_custom_call" | custom-call | tf_op jit(solution)/shard_map/assemble/pallas_call | solution.py:161
  (4 shorter events, 0.1 us)
Async XLA Ops:
  0.6 1.0 %copy-start = (bf16[1,128,768]{2,1,0:T(8,128)(2,1)S(1)}, bf16[1,128,768]{2,1,0:T(8,128)(2,1)}, u32[]{:S(2)}) copy-start(bf16[1,128,768]{2,1,0:T(8,128)(2,1)} %param.8) | copy-start | bytes 589828
  1.7 11.4 %copy-start.6 = (f32[12,257]{1,0:T(8,128)S(1)}, f32[12,257]{1,0:T(8,128)}, u32[]{:S(2)}) copy-start(f32[12,257]{1,0:T(8,128)} %param.11) | copy-start | bytes 37012
  1.7 13.0 %collective-permute-start.1 = (bf16[2,128,768]{2,1,0:T(8,128)(2,1)S(1)}, bf16[2,128,768]{2,1,0:T(8,128)(2,1)S(1)}, u32[]{:S(2)}, u32[]{:S(2)}) collective-permute-start(bf16[2,128,768]{2,1,0:T(8,128)(2,1)S(1)} %constant_dynamic-update-slice_fusion), channel_id=1, source_target_pairs={{1,0},{2,1},{3,2},{4,3},{5,4},{6,5},{7,6},{8,7},{9,8},{10,9},{11,1... | collective-permute-start | bytes 1179656 | tf_op jit(solution)/shard_map/ppermute | solution.py:182
  10.4 6.6 %collective-permute-start = (bf16[2,128,768]{2,1,0:T(8,128)(2,1)S(1)}, bf16[2,128,768]{2,1,0:T(8,128)(2,1)S(1)}, u32[]{:S(2)}, u32[]{:S(2)}) collective-permute-start(bf16[2,128,768]{2,1,0:T(8,128)(2,1)S(1)} %constant_dynamic-update-slice_fusion), channel_id=1, source_target_pairs={{0,1},{1,2},{2,3},{3,4},{4,5},{5,6},{6,7},{7,8},{8,9},{9,10},{10,1... | collective-permute-start | bytes 1179656 | tf_op jit(solution)/shard_map/ppermute | solution.py:181
  14.6 3.2 %copy-start.1 = (bf16[2,128,768]{2,1,0:T(8,128)(2,1)}, bf16[2,128,768]{2,1,0:T(8,128)(2,1)S(1)}, u32[]{:S(2)}) copy-start(bf16[2,128,768]{2,1,0:T(8,128)(2,1)S(1)} %collective-permute-done.1.right_ref) | copy-start | bytes 1179652
  17.1 0.8 copy-start.2
  25.9 20.0 %copy-start.7 = (bf16[2,128,768]{2,1,0:T(8,128)(2,1)S(1)}, bf16[2,128,768]{2,1,0:T(8,128)(2,1)}, u32[]{:S(2)}) copy-start(bf16[2,128,768]{2,1,0:T(8,128)(2,1)} %get-tuple-element.16) | copy-start | bytes 1179652
  27.4 22.6 %all-to-all-start = ((bf16[16,32,128]{2,1,0:T(8,128)(2,1)}), bf16[16,32,128]{2,1,0:T(8,128)(2,1)S(1)}, u32[]{:S(2)}, u32[]{:S(2)}) async-start(bf16[16,32,128]{2,1,0:T(8,128)(2,1)} %broadcast_in_dim.44), calls=%async_computation | async-start | bytes 262144 | tf_op jit(solution)/shard_map/all_to_all | solution.py:171
  38.0 23.0 %collective-permute-start.2 = (bf16[2,128,768]{2,1,0:T(8,128)(2,1)}, bf16[2,128,768]{2,1,0:T(8,128)(2,1)S(1)}, u32[]{:S(2)}, u32[]{:S(2)}) collective-permute-start(bf16[2,128,768]{2,1,0:T(8,128)(2,1)} %get-tuple-element.15), channel_id=1, source_target_pairs={{1,0},{2,1},{3,2},{4,3},{5,4},{6,5},{7,6},{8,7},{9,8},{10,9},{11,1... | collective-permute-start | bytes 1179656 | tf_op jit(solution)/shard_map/ppermute | solution.py:188
  45.9 15.1 %collective-permute-start.3 = (bf16[2,128,768]{2,1,0:T(8,128)(2,1)S(1)}, bf16[2,128,768]{2,1,0:T(8,128)(2,1)S(1)}, u32[]{:S(2)}, u32[]{:S(2)}) collective-permute-start(bf16[2,128,768]{2,1,0:T(8,128)(2,1)S(1)} %copy-done.7), channel_id=1, source_target_pairs={{0,1},{1,2},{2,3},{3,4},{4,5},{5,6},{6,7},{7,8},{8,9},{9,10},{10,1... | collective-permute-start | bytes 1179656 | tf_op jit(solution)/shard_map/ppermute | solution.py:189
  50.7 15.6 %all-to-all-start.1 = ((f32[8,32,128]{2,1,0:T(8,128)}), f32[8,32,128]{2,1,0:T(8,128)S(1)}, u32[]{:S(2)}, u32[]{:S(2)}) async-start(f32[8,32,128]{2,1,0:T(8,128)} %broadcast_in_dim.45), calls=%async_computation.1 | async-start | bytes 262144 | tf_op jit(solution)/shard_map/all_to_all | solution.py:171
  61.1 10.1 %copy-start.3 = (f32[128,768]{1,0:T(8,128)S(1)}, f32[128,768]{1,0:T(8,128)}, u32[]{:S(2)}) copy-start(f32[128,768]{1,0:T(8,128)} %get-tuple-element.14) | copy-start | bytes 1179652
  61.1 10.1 %copy-start.4 = (f32[128,768]{1,0:T(8,128)S(1)}, f32[128,768]{1,0:T(8,128)}, u32[]{:S(2)}) copy-start(f32[128,768]{1,0:T(8,128)} %get-tuple-element.17) | copy-start | bytes 1179652
  67.0 8.7 %all-to-all-start.2 = ((f32[4,32,128]{2,1,0:T(8,128)}), f32[4,32,128]{2,1,0:T(8,128)S(1)}, u32[]{:S(2)}, u32[]{:S(2)}) async-start(f32[4,32,128]{2,1,0:T(8,128)} %broadcast_in_dim.46), calls=%async_computation.2 | async-start | bytes 131072 | tf_op jit(solution)/shard_map/all_to_all | solution.py:171
  75.6 0.6 copy-start.5

commit v2 on v1

v2 whole, which is shorter than its diff:
```python
import functools

import jax
import jax.numpy as jnp
from jax import lax
from jax.experimental import pallas as pl
from jax.experimental.pallas import tpu as pltpu
from jax.sharding import Mesh
from jax.sharding import PartitionSpec as P


H = 12
HD = 64
W = 128
F = 128
D = 768
PAIRS = 6
AXES = ("dp_0", "dp_1", "tm_0", "tm_1", "tm_2")
TM = ("tm_0", "tm_1", "tm_2")
DP = ("dp_0", "dp_1")
Z16 = ("dp_0", "tm_0")
XY = ("dp_1", "tm_1", "tm_2")
NEG = -1e30
ROWS = 32
SCALE = HD**-0.5
UNROLL = (6, 6, 6)
f32 = jnp.float32
bf16 = jnp.bfloat16

NT = (((1,), (1,)), ((), ()))
NN = (((1,), (0,)), ((), ()))


def dot(a, b, dims=NN):
    return lax.dot_general(a, b, dims, preferred_element_type=f32)


def grids():
    row = lax.broadcasted_iota(jnp.int32, (F, F), 0)
    lane = lax.broadcasted_iota(jnp.int32, (F, F), 1)
    return row, lane


def flip_matrix():
    row, lane = grids()
    return jnp.where((row + lane == F) | ((row == 0) & (lane == 0)), 1.0, 0.0).astype(f32)


def flip(rows):
    return lax.dot_general(
        rows, flip_matrix(), NN, precision=lax.Precision.HIGHEST, preferred_element_type=f32
    )


def stacked(info, q, g):
    row, lane = grids()
    low = lane < HD
    zero = jnp.zeros((F, F), bf16)
    q = q * jnp.asarray(SCALE, bf16)
    g = jnp.where(info[0] + row < info[1], g, zero)
    q2 = jnp.concatenate([jnp.where(low, q, zero), jnp.where(low, zero, q)], axis=0)
    g2 = jnp.concatenate([jnp.where(low, g, zero), jnp.where(low, zero, g)], axis=0)
    return q2, g2


def masked_below(bias, start, length):
    pos = start + lax.broadcasted_iota(jnp.int32, bias.shape, 0)
    return jnp.where((pos >= 0) & (pos < length), bias, NEG)


def lanes(pair):
    return pl.ds(pl.multiple_of(pair * F, F), F)


def own_kernel(
    info, q_hbm, g_hbm, table_hbm, kv_ref, s_ref, gp_ref, bias_ref, qg_ref, rt_ref, table_ref, sem
):
    fetch((q_hbm, g_hbm, table_hbm), (qg_ref.at[0], qg_ref.at[1], table_ref), sem)
    first, length, odd = info[0], info[1], info[2]
    row, lane = grids()
    low, high, end = table_ref[:, :F], table_ref[:, F : 2 * F], table_ref[:, 2 * F :]
    at0 = lax.broadcasted_iota(jnp.int32, (H, F), 1) == 0
    rt_ref[0] = jnp.where(at0, high[:, :1], flip(low))
    rt_ref[1] = jnp.where(at0, end, flip(high))
    rt_ref[2] = jnp.broadcast_to(low[:, :1], (H, F))
    below, on = lane < row, lane == row

    def step(pair, carry):
        at = lanes(pair)
        q2, g2 = stacked(info, qg_ref[0, :, at], qg_ref[1, :, at])
        before, own, after = [], [], []
        for h in range(2):
            spread = lambda which: jnp.broadcast_to(rt_ref[which, pl.ds(2 * pair + h, 1), :], (F, F))
            u0 = pltpu.roll(spread(0), 0, 1, stride=1, stride_axis=0)
            u1 = pltpu.roll(spread(1), 0, 1, stride=1, stride_axis=0)
            before.append(jnp.where(below, u0, jnp.where(on, spread(2), NEG)))
            own.append(jnp.where(below, u1, u0))
            after.append(jnp.where(below, NEG, u1))
        before, own, after = (jnp.concatenate(b, axis=1) for b in (before, own, after))
        bias_ref[1 - odd, pair] = masked_below(before, first - W, length)
        bias_ref[odd, pair] = masked_below(after, first + W, length)
        s_ref[pair] = dot(kv_ref[0, :, at], q2, NT) + masked_below(own, first, length)
        gp_ref[pair] = dot(kv_ref[1, :, at], g2, NT)
        return carry

    lax.fori_loop(0, PAIRS, step, 0, unroll=UNROLL[0])


def rows_kernel(
    info, a_ref, b_ref, s_ref, gp_ref, bias_ref, qg_ref, p_ref, ds_ref, gb_ref, acc_ref, diag_ref,
):
    odd = info[2] == 1
    row, lane = grids()
    below, on = lane < row, lane == row

    def step(pair, carry):
        at = lanes(pair)
        q2, g2 = stacked(info, qg_ref[0, :, at], qg_ref[1, :, at])
        scores = [
            dot(a_ref[0, :, at], q2, NT) + bias_ref[0, pair],
            s_ref[pair],
            dot(b_ref[0, :, at], q2, NT) + bias_ref[1, pair],
        ]
        top = functools.reduce(jnp.maximum, [jnp.max(s, axis=0, keepdims=True) for s in scores])
        exps = [jnp.exp(s - top) for s in scores]
        total = functools.reduce(jnp.add, [jnp.sum(e, axis=0, keepdims=True) for e in exps])
        inverse = 1.0 / total
        probs = [e * inverse for e in exps]
        gp = [dot(a_ref[1, :, at], g2, NT), gp_ref[pair], dot(b_ref[1, :, at], g2, NT)]
        delta = functools.reduce(
            jnp.add, [jnp.sum(p * d, axis=0, keepdims=True) for p, d in zip(probs, gp)]
        )
        ds = [p * (d - delta) for p, d in zip(probs, gp)]
        for i in range(3):
            p_ref[pair, i * F : (i + 1) * F] = probs[i].astype(bf16)
            ds_ref[pair, i * F : (i + 1) * F] = ds[i].astype(bf16)
        for h in range(2):
            side_a, mid, side_b = (d[:, h * F : (h + 1) * F] for d in ds)
            before = jnp.where(odd, side_a, side_b)
            after = jnp.where(odd, side_b, side_a)
            y1 = jnp.where(below, before, mid)
            y2 = jnp.where(below, mid, after)
            for y, spot in ((y1, 2 * pair + h), (y2, H + 2 * pair + h)):
                total_y = y[:8]
                for k in range(1, 16):
                    total_y = total_y + pltpu.roll(y[8 * k : 8 * k + 8], F - 8 * k, 1)
                acc_ref[spot] = total_y
            diag_ref[2 * pair + h] = jnp.sum(jnp.where(on, before, 0.0), axis=0, keepdims=True)
        return carry

    lax.fori_loop(0, PAIRS, step, 0, unroll=UNROLL[1])
    summed = acc_ref[:, 0, :]
    for s in range(1, 8):
        summed = summed + pltpu.roll(acc_ref[:, s, :], F - s, 1)
    turned = flip(summed)
    head = lax.broadcasted_iota(jnp.int32, (H, F), 0)
    at = lax.broadcasted_iota(jnp.int32, (H, F), 1)
    zed = jnp.sum(diag_ref[:, 0, :], axis=1, keepdims=True)
    one, two = turned[:H], turned[H:]
    last = jnp.sum(jnp.where(head == at, two[:, :1], 0.0), axis=0, keepdims=True)
    packed = jnp.concatenate(
        [
            jnp.where(at == 0, zed, one),
            jnp.where(at == 0, one[:, :1], two),
            jnp.broadcast_to(last, (ROWS - 2 * H, F)),
        ],
        axis=0,
    ).astype(bf16)
    for i in range(gb_ref.shape[0]):
        gb_ref[i] = packed


def outputs_kernel(
    info, q_hbm, g_hbm, k_hbm, v_hbm, a_hbm, b_hbm, p_ref, ds_ref,
    ctx_ref, dq_ref, dk_ref, dv_ref, da_ref, db_ref, held, a_ref, b_ref, sem,
):
    fetch(
        (q_hbm, g_hbm, k_hbm, v_hbm, a_hbm, b_hbm),
        [held.at[i] for i in range(4)] + [a_ref, b_ref],
        sem,
    )
    row, _ = grids()
    valid = info[0] + row < info[1]

    def step(pair, carry):
        at = lanes(pair)
        q2, g2 = stacked(info, held[0, :, at], held[1, :, at])
        p, ds = p_ref[pair], ds_ref[pair]
        keys = jnp.concatenate([a_ref[0, :, at], held[2, :, at], b_ref[0, :, at]], axis=0)
        values = jnp.concatenate([a_ref[1, :, at], held[3, :, at], b_ref[1, :, at]], axis=0)
        dk = dot(ds, q2)
        dv = dot(p, g2)
        da_ref[0, :, at] = dk[:F].astype(bf16)
        da_ref[1, :, at] = dv[:F].astype(bf16)
        dk_ref[:, at] = dk[F : 2 * F]
        dv_ref[:, at] = dv[F : 2 * F]
        db_ref[0, :, at] = dk[2 * F :].astype(bf16)
        db_ref[1, :, at] = dv[2 * F :].astype(bf16)
        ctx_t = dot(jnp.transpose(values), p)
        dq_t = dot(jnp.transpose(keys), ds)
        ctx = jnp.transpose(jnp.concatenate([ctx_t[:HD, :F], ctx_t[HD:, F:]], axis=0))
        ctx_ref[:, at] = jnp.where(valid, ctx, 0.0).astype(bf16)
        dq = jnp.transpose(jnp.concatenate([dq_t[:HD, :F], dq_t[HD:, F:]], axis=0))
        dq_ref[:, at] = (dq * SCALE).astype(bf16)
        return carry

    lax.fori_loop(0, PAIRS, step, 0, unroll=UNROLL[2])


def fetch(sources, targets, sem):
    copies = [
        pltpu.make_async_copy(source, target, sem.at[i])
        for i, (source, target) in enumerate(zip(sources, targets))
    ]
    for copy in copies:
        copy.start()
    for copy in copies:
        copy.wait()


def stack_kernel(k_ref, v_ref, out_ref, sem):
    fetch((k_ref, v_ref), (out_ref.at[0], out_ref.at[1]), sem)


def stack(k, v):
    return pl.pallas_call(
        stack_kernel,
        in_specs=[pl.BlockSpec(memory_space=pltpu.HBM)] * 2,
        out_specs=pl.BlockSpec(memory_space=pltpu.VMEM),
        out_shape=shape(bf16, 2, F, D),
        scratch_shapes=[pltpu.SemaphoreType.DMA((2,))],
        compiler_params=pltpu.CompilerParams(vmem_limit_bytes=1 << 20),
        name="stack",
    )(k, v)


def in_vmem(kernel, far, args, out_shape, scratch, flops):
    vmem = pl.BlockSpec(memory_space=pltpu.VMEM)
    hbm = pl.BlockSpec(memory_space=pltpu.HBM)
    return pl.pallas_call(
        kernel,
        in_specs=[pl.BlockSpec(memory_space=pltpu.SMEM)]
        + [hbm] * far
        + [vmem] * (len(args) - 1 - far),
        out_specs=[vmem] * len(out_shape),
        out_shape=out_shape,
        scratch_shapes=scratch,
        compiler_params=pltpu.CompilerParams(vmem_limit_bytes=16 << 20),
        cost_estimate=pl.CostEstimate(flops=flops, bytes_accessed=4 << 20, transcendentals=0),
    )(*args)


def shape(dtype, *dims):
    return jax.ShapeDtypeStruct(dims, dtype)


def own_part(*args):
    return in_vmem(
        own_kernel, 3, args,
        [shape(f32, PAIRS, F, 2 * F)] * 2
        + [shape(f32, 2, PAIRS, F, 2 * F), shape(bf16, 2, F, D)],
        [
            pltpu.VMEM((3, H, F), f32),
            pltpu.VMEM((H, 2 * W + 1), f32),
            pltpu.SemaphoreType.DMA((3,)),
        ],
        1 << 30,
    )


def row_part(copies, *args):
    return in_vmem(
        rows_kernel, 0, args,
        [shape(bf16, PAIRS, 3 * F, 2 * F)] * 2 + [shape(bf16, copies, ROWS, F)],
        [pltpu.VMEM((2 * H, 8, F), f32), pltpu.VMEM((H, 1, F), f32)], 1 << 30,
    )


def output_part(*args):
    return in_vmem(
        outputs_kernel, 6, args,
        [shape(bf16, F, D)] * 2 + [shape(f32, F, D)] * 2 + [shape(bf16, 2, F, D)] * 2,
        [pltpu.VMEM((4, F, D), bf16)]
        + [pltpu.VMEM((2, F, D), bf16)] * 2
        + [pltpu.SemaphoreType.DMA((6,))],
        1 << 30,
    )


def finish_kernel(dk_ref, dv_ref, a_ref, b_ref, gk_ref, gv_ref):
    for i, (own, out) in enumerate(((dk_ref, gk_ref), (dv_ref, gv_ref))):
        out[...] = (own[...] + a_ref[i].astype(f32) + b_ref[i].astype(f32)).astype(bf16)


def finish(dk, dv, a, b):
    vmem = pl.BlockSpec(memory_space=pltpu.VMEM)
    return pl.pallas_call(
        finish_kernel,
        in_specs=[vmem] * 4,
        out_shape=[shape(bf16, F, D)] * 2,
        compiler_params=pltpu.CompilerParams(vmem_limit_bytes=16 << 20),
        name="finish",
    )(dk, dv, a, b)


def size_of(axes):
    count = 1
    for axis in axes:
        count *= lax.axis_size(axis)
    return count


def step(query_proj, key_proj, value_proj, cotangent, lengths, rel_bias):
    ends = size_of(TM)
    at = lax.axis_index(TM)
    info = jnp.stack([at * F, lengths[0], at & 1]).astype(jnp.int32)
    near = [(i, i ^ 1) for i in range(ends)]
    far = [(i, i + 1 if i % 2 else i - 1) for i in range(1, ends - 1)]
    stay = lambda x: pltpu.with_memory_space_constraint(x, pltpu.HBM)
    q, k, v, g = (stay(x[0]) for x in (query_proj, key_proj, value_proj, cotangent))
    rel_bias = stay(rel_bias)
    kv = stack(k, v)
    side_b = lax.ppermute(kv, TM, far)
    side_a = lax.ppermute(kv, TM, near)
    s, gp, bias, qg = own_part(info, q, g, rel_bias, kv)
    p, ds, gb = row_part(size_of(Z16), info, side_a, side_b, s, gp, bias, qg)
    z = lax.all_to_all(gb, Z16, 0, 0, tiled=True)
    ctx, dq, dk, dv, da, db = output_part(info, q, g, k, v, stay(side_a), stay(side_b), p, ds)
    from_b = lax.ppermute(db, TM, far)
    from_a = lax.ppermute(da, TM, near)
    z = jnp.sum(z.astype(f32), axis=0).astype(bf16)
    z = jnp.broadcast_to(z[None], (size_of(XY), ROWS, F))
    z = lax.all_to_all(z, XY, 0, 0, tiled=True)
    z = jnp.sum(z.astype(f32), axis=0)
    grad_bias = jnp.concatenate([z[:H], z[H : 2 * H], z[2 * H, :H, None]], axis=1)
    grad_key, grad_value = finish(dk, dv, from_a, from_b)
    return ctx[None], dq[None], grad_key[None], grad_value[None], grad_bias


def solution(mesh):
    finer = Mesh(mesh.devices.reshape(2, 4, 8, 4, 2), AXES)
    in_specs = (P(DP, TM, None), P(DP, TM, None), P(DP, TM, None), P(DP, TM, None), P(DP), P())
    out_specs = (P(DP, TM, None), P(DP, TM, None), P(DP, TM, None), P(DP, TM, None), P())
    return jax.shard_map(step, mesh=finer, in_specs=in_specs, out_specs=out_specs, check_vma=False)
```

time: 78.9 us -> 64.8 us (0.82)
  starting transfers between devices: 45.7 us -> 38 us
  local copies, waits for them, and re-layouts: 5.37 us -> 0.84 us
  waiting for transfers between devices: 13.4 us -> 10.3 us
  Pallas kernels: 9.61 us -> 12.1 us
    ppermute x4, starting transfers between devices: 20.5 us -> 15 us  [the longest x1 4.93 us: step(): side_a = lax.ppermute(kv, TM, near)]
    pallas_call x2 -> x5, Pallas kernels: 9.61 us -> 12.1 us  [the longest x3 10.3 us: in_vmem(): pl.pallas_call(kernel, in_specs=[pl.BlockSpec(memory_space=pltpu.SMEM)] +...]
    ppermute x4, waiting for transfers between devices: 2.43 us -> 0.01 us  [the longest x1 0.01 us: step(): side_b = lax.ppermute(kv, TM, far)]
    all_to_all x3 -> x2, starting transfers between devices: 25.2 us -> 22.9 us  [the longest x1 13 us: step(): z = lax.all_to_all(gb, Z16, 0, 0, tiled=True)]
    broadcast_in_dim x4 -> x1, local copies, waits for them, and re-layouts: 2.7 us -> 0.73 us  [step(): z = jnp.broadcast_to(z[None], (size_of(XY), ROWS, F))]
    unnamed x17 -> x4, local copies, waits for them, and re-layouts: 1.68 us -> 0.01 us
    reduce_sum x2, other arithmetic: 0.04 us -> 0.98 us  [the longest x1 0.93 us: step(): z = jnp.sum(z.astype(f32), axis=0).astype(bf16)]
    broadcast_in_dim x1 -> x0, other arithmetic: 0.81 us -> none  [on_device(): return (ctx[None], dq[None], grad_key[None], grad_value[None], grad_bias)]
  transfers between devices with their start and end apart: 7 -> 6, of which waited for: 4 -> 2; matrix products, arithmetic and copies ran while one was open for 4% -> 3% of each run, Pallas kernels for 0% -> 12%
where the time goes in v2:
time: 64.8 us; the launch traced here: 64.3 us
  starting transfers between devices  38 us (59%)
  Pallas kernels  12.1 us (19%)
  waiting for transfers between devices  10.3 us (16%)
  other arithmetic  1.67 us (3%)
  between operations  1.43 us (2%)
  local copies, waits for them, and re-layouts  0.84 us (1%)
    all_to_all x1, starting transfers between devices, step(): z = lax.all_to_all(gb, Z16, 0, 0, tiled=True)  13 us
    pallas_call x3, Pallas kernels, in_vmem(): pl.pallas_call(kernel, in_specs=[pl.BlockSpec(memory_space=pltpu.SMEM)] +...  10.3 us
    all_to_all x1, starting transfers between devices, step(): z = lax.all_to_all(z, XY, 0, 0, tiled=True)  9.88 us
    all_to_all x1, waiting for transfers between devices, step(): z = lax.all_to_all(z, XY, 0, 0, tiled=True)  8.04 us
    ppermute x1, starting transfers between devices, step(): side_a = lax.ppermute(kv, TM, near)  4.93 us
    ppermute x1, starting transfers between devices, step(): side_b = lax.ppermute(kv, TM, far)  4.5 us
    ppermute x1, starting transfers between devices, step(): from_a = lax.ppermute(da, TM, near)  3.69 us
    all_to_all x1, waiting for transfers between devices, step(): z = lax.all_to_all(gb, Z16, 0, 0, tiled=True)  2.22 us
  transfers between devices with their start and end apart: 6, of which 2 were waited for; matrix products, arithmetic and copies ran while one was open for 3% of the time, Pallas kernels for 12%

profile of v2, /device:TPU:1, one launch (start us, length us, event | category | flops | bytes accessed | tf_op | source)
XLA Modules:
  0.0 64.3 jit_solution(12336774034667548782)
XLA Ops:
  0.6 1.0 %stack.13.kv_ref = bf16[2,128,768]{2,1,0:T(8,128)(2,1)S(1)} custom-call(bf16[128,768]{1,0:T(8,128)(2,1)} %bitcast.12, bf16[128,768]{1,0:T(8,128)(2,1)} %bitcast.14), custom_call_target="tpu_custom_call" | custom-call | tf_op jit(solution)/shard_map/stack/pallas_call | solution.py:226
  1.7 4.5 %collective-permute-start.1 = (bf16[2,128,768]{2,1,0:T(8,128)(2,1)S(1)}, bf16[2,128,768]{2,1,0:T(8,128)(2,1)S(1)}, u32[]{:S(2)}, u32[]{:S(2)}) collective-permute-start(bf16[2,128,768]{2,1,0:T(8,128)(2,1)S(1)} %stack.13.kv_ref), channel_id=1, source_target_pairs={{1,2},{2,1},{3,4},{4,3},{5,6},{6,5},{7,8},{8,7},{9,10},{10,9},{11,... | collective-permute-start | bytes 1179656 | tf_op jit(solution)/shard_map/ppermute | solution.py:323
  6.2 4.9 %collective-permute-start = (bf16[2,128,768]{2,1,0:T(8,128)(2,1)S(1)}, bf16[2,128,768]{2,1,0:T(8,128)(2,1)S(1)}, u32[]{:S(2)}, u32[]{:S(2)}) collective-permute-start(bf16[2,128,768]{2,1,0:T(8,128)(2,1)S(1)} %stack.13.kv_ref), channel_id=1, source_target_pairs={{0,1},{1,0},{2,3},{3,2},{4,5},{5,4},{6,7},{7,6},{8,9},{9,8},{10,11... | collective-permute-start | bytes 1179656 | tf_op jit(solution)/shard_map/ppermute | solution.py:324
  11.8 0.1 pad_add_fusion.info
  11.9 2.5 %shard_map.101 = (f32[6,128,256]{2,1,0:T(8,128)S(1)}, f32[6,128,256]{2,1,0:T(8,128)S(1)}, f32[2,6,128,256]{3,2,1,0:T(8,128)S(1)}, bf16[2,128,768]{2,1,0:T(8,128)(2,1)S(1)}) custom-call(s32[3]{0:T(128)S(1)} %pad_add_fusion.info, bf16[128,768]{1,0:T(8,128)(2,1)} %bitcast.16, bf16[128,768]{1,0:T(8,128)(2,1)} %bitcast.18, f32[12,257]{1,0:T(8,128)} %table_hbm.1, ...), custom_call_target="tpu_custom_call" | custom-call | flops 1073741824 | bytes 4194304 | tf_op jit(solution)/shard_map/pallas_call | solution.py:240
  14.3 0.0 collective-permute-done.1.b_ref.b_hbm
  14.3 0.0 copy-start
  14.3 0.0 collective-permute-done.a_ref.a_hbm
  14.3 0.0 copy-start.1
  14.4 3.6 %shard_map.102 = (bf16[6,384,256]{2,1,0:T(8,128)(2,1)S(1)}, bf16[6,384,256]{2,1,0:T(8,128)(2,1)S(1)}, bf16[16,32,128]{2,1,0:T(8,128)(2,1)}) custom-call(s32[3]{0:T(128)S(1)} %pad_add_fusion.info, bf16[2,128,768]{2,1,0:T(8,128)(2,1)S(1)} %collective-permute-done.a_ref.a_hbm, bf16[2,128,768]{2,1,0:T(8,128)(2,1)S(1)} %collective-permute-done.1.b_ref.b_hbm, ...), custom_call_target="tpu_custom_call" | custom-call | flops 1073741824 | bytes 4194304 | tf_op jit(solution)/shard_map/pallas_call | solution.py:240
  18.0 0.0 copy-done
  18.0 0.0 copy-done.1
  18.0 13.0 %all-to-all-start = ((bf16[16,32,128]{2,1,0:T(8,128)(2,1)}), bf16[16,32,128]{2,1,0:T(8,128)(2,1)}, u32[]{:S(2)}, u32[]{:S(2)}) async-start(bf16[16,32,128]{2,1,0:T(8,128)(2,1)} %get-tuple-element.34), calls=%async_computation | async-start | bytes 262144 | tf_op jit(solution)/shard_map/all_to_all | solution.py:327
  31.1 4.2 %shard_map.103 = (bf16[128,768]{1,0:T(8,128)(2,1)}, bf16[128,768]{1,0:T(8,128)(2,1)}, f32[128,768]{1,0:T(8,128)S(1)}, f32[128,768]{1,0:T(8,128)S(1)}, bf16[2,128...) custom-call(s32[3]{0:T(128)S(1)} %pad_add_fusion.info, bf16[128,768]{1,0:T(8,128)(2,1)} %bitcast.17, ...), custom_call_target="tpu_custom_call" | custom-call | flops 1073741824 | bytes 4194304 | tf_op jit(solution)/shard_map/pallas_call | solution.py:240
  35.3 3.7 %collective-permute-start.2 = (bf16[2,128,768]{2,1,0:T(8,128)(2,1)}, bf16[2,128,768]{2,1,0:T(8,128)(2,1)S(1)}, u32[]{:S(2)}, u32[]{:S(2)}) collective-permute-start(bf16[2,128,768]{2,1,0:T(8,128)(2,1)} %get-tuple-element.30), channel_id=1, source_target_pairs={{0,1},{1,0},{2,3},{3,2},{4,5},{5,4},{6,7},{7,6},{8,9},{9,8},{10,11... | collective-permute-start | bytes 1179656 | tf_op jit(solution)/shard_map/ppermute | solution.py:330
  39.0 1.9 %collective-permute-start.3 = (bf16[2,128,768]{2,1,0:T(8,128)(2,1)}, bf16[2,128,768]{2,1,0:T(8,128)(2,1)S(1)}, u32[]{:S(2)}, u32[]{:S(2)}) collective-permute-start(bf16[2,128,768]{2,1,0:T(8,128)(2,1)} %get-tuple-element.31), channel_id=1, source_target_pairs={{1,2},{2,1},{3,4},{4,3},{5,6},{6,5},{7,8},{8,7},{9,10},{10,9},{11,... | collective-permute-start | bytes 1179656 | tf_op jit(solution)/shard_map/ppermute | solution.py:329
  40.9 2.2 %all-to-all-done = bf16[16,32,128]{2,1,0:T(8,128)(2,1)} async-done(((bf16[16,32,128]{2,1,0:T(8,128)(2,1)}), bf16[16,32,128]{2,1,0:T(8,128)(2,1)}, u32[]{:S(2)}, u32[]{:S(2)}) %all-to-all-start) | async-done | bytes 131104 | tf_op jit(solution)/shard_map/all_to_all | solution.py:327
  43.1 0.9 %reduce_sum.21 = bf16[32,128]{1,0:T(8,128)(2,1)S(1)} reduce(bf16[16,32,128]{2,1,0:T(8,128)(2,1)} %all-to-all-done, bf16[]{:T(256)} %constant.22.clone.1), dimensions={0}, to_apply=%region_0.0 | reduce | flops 61440 | bytes 139266 | tf_op jit(solution)/shard_map/reduce_sum | solution.py:331
  44.1 0.7 %broadcast_in_dim.22 = bf16[32,32,128]{2,1,0:T(8,128)(2,1)} broadcast(bf16[32,128]{1,0:T(8,128)(2,1)S(1)} %reduce_sum.21), dimensions={1,2} | broadcast | bytes 270336 | tf_op jit(solution)/shard_map/broadcast_in_dim | solution.py:332
  44.8 9.9 %all-to-all-start.1 = ((bf16[32,32,128]{2,1,0:T(8,128)(2,1)}), bf16[32,32,128]{2,1,0:T(8,128)(2,1)S(1)}, u32[]{:S(2)}, u32[]{:S(2)}) async-start(bf16[32,32,128]{2,1,0:T(8,128)(2,1)} %broadcast_in_dim.22), calls=%async_computation.1 | async-start | bytes 524288 | tf_op jit(solution)/shard_map/all_to_all | solution.py:333
  54.7 0.0 collective-permute-done.2.a_ref
  54.7 0.0 collective-permute-done.3.b_ref
  54.7 0.8 %finish.1 = (bf16[128,768]{1,0:T(8,128)(2,1)}, bf16[128,768]{1,0:T(8,128)(2,1)}) custom-call(f32[128,768]{1,0:T(8,128)S(1)} %get-tuple-element.28.dk_ref, f32[128,768]{1,0:T(8,128)S(1)} %get-tuple-element.29.dv_ref, bf16[2,128,768]{2,1,0:T(8,128)(2,1)S(1)} %collective-permute-done.2.a_ref, bf16[2,128,768]{2,1,0:T(8,128)(2,1)S(1)} %collective-permute-done.3.b_ref), custom_call_target="tpu_custom_call" | custom-call | tf_op jit(solution)/shard_map/finish/pallas_call | solution.py:297
  55.5 8.0 %all-to-all-done.1 = bf16[32,32,128]{2,1,0:T(8,128)(2,1)S(1)} async-done(((bf16[32,32,128]{2,1,0:T(8,128)(2,1)}), bf16[32,32,128]{2,1,0:T(8,128)(2,1)S(1)}, u32[]{:S(2)}, u32[]{:S(2)}) %all-to-all-start.1) | async-done | bytes 262176 | tf_op jit(solution)/shard_map/all_to_all | solution.py:333
  63.6 0.1 copy.12
  63.7 0.6 pad_maximum_fusion
  (3 shorter events, 0.1 us)
Async XLA Ops:
  1.7 12.6 %collective-permute-start.1 = (bf16[2,128,768]{2,1,0:T(8,128)(2,1)S(1)}, bf16[2,128,768]{2,1,0:T(8,128)(2,1)S(1)}, u32[]{:S(2)}, u32[]{:S(2)}) collective-permute-start(bf16[2,128,768]{2,1,0:T(8,128)(2,1)S(1)} %stack.13.kv_ref), channel_id=1, source_target_pairs={{1,2},{2,1},{3,4},{4,3},{5,6},{6,5},{7,8},{8,7},{9,10},{10,9},{11,... | collective-permute-start | bytes 1179656 | tf_op jit(solution)/shard_map/ppermute | solution.py:323
  6.2 8.2 %collective-permute-start = (bf16[2,128,768]{2,1,0:T(8,128)(2,1)S(1)}, bf16[2,128,768]{2,1,0:T(8,128)(2,1)S(1)}, u32[]{:S(2)}, u32[]{:S(2)}) collective-permute-start(bf16[2,128,768]{2,1,0:T(8,128)(2,1)S(1)} %stack.13.kv_ref), channel_id=1, source_target_pairs={{0,1},{1,0},{2,3},{3,2},{4,5},{5,4},{6,7},{7,6},{8,9},{9,8},{10,11... | collective-permute-start | bytes 1179656 | tf_op jit(solution)/shard_map/ppermute | solution.py:324
  14.3 3.7 %copy-start = (bf16[2,128,768]{2,1,0:T(8,128)(2,1)}, bf16[2,128,768]{2,1,0:T(8,128)(2,1)S(1)}, u32[]{:S(2)}) copy-start(bf16[2,128,768]{2,1,0:T(8,128)(2,1)S(1)} %collective-permute-done.1.b_ref.b_hbm) | copy-start | bytes 1179652
  14.3 3.7 %copy-start.1 = (bf16[2,128,768]{2,1,0:T(8,128)(2,1)}, bf16[2,128,768]{2,1,0:T(8,128)(2,1)S(1)}, u32[]{:S(2)}) copy-start(bf16[2,128,768]{2,1,0:T(8,128)(2,1)S(1)} %collective-permute-done.a_ref.a_hbm) | copy-start | bytes 1179652
  18.0 25.1 %all-to-all-start = ((bf16[16,32,128]{2,1,0:T(8,128)(2,1)}), bf16[16,32,128]{2,1,0:T(8,128)(2,1)}, u32[]{:S(2)}, u32[]{:S(2)}) async-start(bf16[16,32,128]{2,1,0:T(8,128)(2,1)} %get-tuple-element.34), calls=%async_computation | async-start | bytes 262144 | tf_op jit(solution)/shard_map/all_to_all | solution.py:327
  35.3 19.4 %collective-permute-start.2 = (bf16[2,128,768]{2,1,0:T(8,128)(2,1)}, bf16[2,128,768]{2,1,0:T(8,128)(2,1)S(1)}, u32[]{:S(2)}, u32[]{:S(2)}) collective-permute-start(bf16[2,128,768]{2,1,0:T(8,128)(2,1)} %get-tuple-element.30), channel_id=1, source_target_pairs={{0,1},{1,0},{2,3},{3,2},{4,5},{5,4},{6,7},{7,6},{8,9},{9,8},{10,11... | collective-permute-start | bytes 1179656 | tf_op jit(solution)/shard_map/ppermute | solution.py:330
  39.0 15.7 %collective-permute-start.3 = (bf16[2,128,768]{2,1,0:T(8,128)(2,1)}, bf16[2,128,768]{2,1,0:T(8,128)(2,1)S(1)}, u32[]{:S(2)}, u32[]{:S(2)}) collective-permute-start(bf16[2,128,768]{2,1,0:T(8,128)(2,1)} %get-tuple-element.31), channel_id=1, source_target_pairs={{1,2},{2,1},{3,4},{4,3},{5,6},{6,5},{7,8},{8,7},{9,10},{10,9},{11,... | collective-permute-start | bytes 1179656 | tf_op jit(solution)/shard_map/ppermute | solution.py:329
  44.8 18.8 %all-to-all-start.1 = ((bf16[32,32,128]{2,1,0:T(8,128)(2,1)}), bf16[32,32,128]{2,1,0:T(8,128)(2,1)S(1)}, u32[]{:S(2)}, u32[]{:S(2)}) async-start(bf16[32,32,128]{2,1,0:T(8,128)(2,1)} %broadcast_in_dim.22), calls=%async_computation.1 | async-start | bytes 524288 | tf_op jit(solution)/shard_map/all_to_all | solution.py:333

commit v3 on v2

v3 whole, which is shorter than its diff:
```python
import jax
import jax.numpy as jnp
from jax import lax
from jax.experimental import pallas as pl
from jax.experimental.pallas import tpu as pltpu
from jax.sharding import Mesh
from jax.sharding import PartitionSpec as P


H = 12
HD = 64
W = 128
F = 128
D = 768
PAIRS = 6
AXES = ("dp_0", "dp_1", "tm_0", "tm_1", "tm_2")
TM = ("tm_0", "tm_1", "tm_2")
DP = ("dp_0", "dp_1")
Z16 = ("dp_0", "tm_0")
XY = ("dp_1", "tm_1", "tm_2")
NEG = -1e30
ROWS = 32
SCALE = HD**-0.5
f32 = jnp.float32
bf16 = jnp.bfloat16

NT = (((1,), (1,)), ((), ()))
NN = (((1,), (0,)), ((), ()))


def dot(a, b, dims=NN):
    return lax.dot_general(a, b, dims, preferred_element_type=f32)


def grids():
    row = lax.broadcasted_iota(jnp.int32, (F, F), 0)
    lane = lax.broadcasted_iota(jnp.int32, (F, F), 1)
    return row, lane


def flip_matrix():
    row, lane = grids()
    return jnp.where((row + lane == F) | ((row == 0) & (lane == 0)), 1.0, 0.0).astype(f32)


def flip(rows):
    return lax.dot_general(
        rows, flip_matrix(), NN, precision=lax.Precision.HIGHEST, preferred_element_type=f32
    )


def position(length_ref):
    at = lax.axis_index(TM)
    return at * F, length_ref[0], at & 1


def stacked(info, q, g):
    row, lane = grids()
    low = lane < HD
    zero = jnp.zeros((F, F), bf16)
    q = q * jnp.asarray(SCALE, bf16)
    g = jnp.where(info[0] + row < info[1], g, zero)
    q2 = jnp.concatenate([jnp.where(low, q, zero), jnp.where(low, zero, q)], axis=0)
    g2 = jnp.concatenate([jnp.where(low, g, zero), jnp.where(low, zero, g)], axis=0)
    return q2, g2


def lanes(pair):
    return pl.ds(pl.multiple_of(pair * F, F), F)


def twice(x):
    return jnp.concatenate([x, x], axis=1)


def own_kernel(
    length_ref, q_hbm, g_hbm, k_hbm, v_hbm, table_hbm,
    s_ref, gp_ref, bias_ref, edge_ref, qg_ref, rt_ref, table_ref, kv_ref, sem,
):
    fetch(
        (q_hbm, g_hbm, k_hbm, v_hbm, table_hbm),
        (qg_ref.at[0], qg_ref.at[1], kv_ref.at[0], kv_ref.at[1], table_ref),
        sem,
    )
    info = position(length_ref)
    first, length = info[0], info[1]
    row, lane = grids()
    low, high, end = table_ref[:, :F], table_ref[:, F : 2 * F], table_ref[:, 2 * F :]
    at0 = lax.broadcasted_iota(jnp.int32, (H, F), 1) == 0
    rt_ref[0] = jnp.where(at0, high[:, :1], flip(low))
    rt_ref[1] = jnp.where(at0, end, flip(high))
    rt_ref[2] = jnp.broadcast_to(low[:, :1], (H, F))
    below = lane < row
    here = (first + row) < length
    around = jnp.where(below, first - W + row, first + W + row)
    around = (around >= 0) & (around < length)
    edge = first - W + lane[:1]
    edge = (edge >= 0) & (edge < length)

    def step(pair, carry):
        at = lanes(pair)
        q2, g2 = stacked(info, qg_ref[0, :, at], qg_ref[1, :, at])
        own, other, ends = [], [], []
        for h in range(2):
            line = lambda which: rt_ref[which, pl.ds(2 * pair + h, 1), :]
            spread = lambda which: jnp.broadcast_to(line(which), (F, F))
            u0 = pltpu.roll(spread(0), 0, 1, stride=1, stride_axis=0)
            u1 = pltpu.roll(spread(1), 0, 1, stride=1, stride_axis=0)
            own.append(jnp.where(here, jnp.where(below, u1, u0), NEG))
            other.append(jnp.where(around, jnp.where(below, u0, u1), NEG))
            ends.append(jnp.where(edge, line(2), NEG))
        bias_ref[pair] = jnp.concatenate(other, axis=1)
        edge_ref[pair] = jnp.concatenate(ends, axis=1)
        s_ref[pair] = dot(kv_ref[0, :, at], q2, NT) + jnp.concatenate(own, axis=1)
        gp_ref[pair] = dot(kv_ref[1, :, at], g2, NT)
        return carry

    lax.fori_loop(0, PAIRS, step, 0, unroll=PAIRS)


def rows_kernel(
    length_ref, ak_ref, av_ref, bk_ref, bv_ref, s_ref, gp_ref, bias_ref, edge_ref, qg_ref,
    p_ref, ds_ref, p0_ref, ds0_ref, gb_ref, acc_ref,
):
    info = position(length_ref)
    row, lane = grids()
    below, on = lane < row, lane == row
    below2, on2 = twice(below), twice(on)

    def run(before_refs, after_refs):
        for pair in range(PAIRS):
            at = pl.ds(pair * F, F)
            q2, g2 = stacked(info, qg_ref[0, :, at], qg_ref[1, :, at])

            def around(which, rows2):
                left = dot(before_refs[which][:, at], rows2, NT)
                right = dot(after_refs[which][:, at], rows2, NT)
                edge = jnp.sum(jnp.where(on2, left, 0.0), axis=0, keepdims=True)
                return jnp.where(below2, left, right), edge

            s1, s0 = around(0, q2)
            s1, s0, s2 = s1 + bias_ref[pair], s0 + edge_ref[pair], s_ref[pair]
            top = jnp.maximum(jnp.max(jnp.maximum(s1, s2), axis=0, keepdims=True), s0)
            e0, e1, e2 = jnp.exp(s0 - top), jnp.exp(s1 - top), jnp.exp(s2 - top)
            inverse = 1.0 / (e0 + jnp.sum(e1 + e2, axis=0, keepdims=True))
            p0, p1, p2 = e0 * inverse, e1 * inverse, e2 * inverse
            g1, g0 = around(1, g2)
            g2_own = gp_ref[pair]
            delta = p0 * g0 + jnp.sum(p1 * g1 + p2 * g2_own, axis=0, keepdims=True)
            d0, d1, d2 = p0 * (g0 - delta), p1 * (g1 - delta), p2 * (g2_own - delta)
            p_ref[pair, 0], p_ref[pair, 1] = p1.astype(bf16), p2.astype(bf16)
            ds_ref[pair, 0], ds_ref[pair, 1] = d1.astype(bf16), d2.astype(bf16)
            p0_ref[pair], ds0_ref[pair] = p0, d0
            for h in range(2):
                part = slice(h * F, (h + 1) * F)
                y1 = jnp.where(below, d1[:, part], d2[:, part])
                y2 = jnp.where(below, d2[:, part], d1[:, part])
                for y, spot in ((y1, 2 * pair + h), (y2, H + 2 * pair + h)):
                    total_y = y[:8]
                    for k in range(1, 16):
                        total_y = total_y + pltpu.roll(y[8 * k : 8 * k + 8], F - 8 * k, 1)
                    acc_ref[spot] = total_y

    @pl.when(info[2] == 1)
    def _():
        run((ak_ref, av_ref), (bk_ref, bv_ref))

    @pl.when(info[2] == 0)
    def _():
        run((bk_ref, bv_ref), (ak_ref, av_ref))

    summed = acc_ref[:, 0, :]
    for s in range(1, 8):
        summed = summed + pltpu.roll(acc_ref[:, s, :], F - s, 1)
    turned = flip(summed)
    head = lax.broadcasted_iota(jnp.int32, (H, F), 0)
    at = lax.broadcasted_iota(jnp.int32, (H, F), 1)
    edges = ds0_ref[:, 0, :]
    zed = jnp.concatenate(
        [
            jnp.sum(edges[pair : pair + 1, h * F : (h + 1) * F], axis=1, keepdims=True)
            for pair in range(PAIRS)
            for h in range(2)
        ],
        axis=0,
    )
    one, two = turned[:H], turned[H:]
    last = jnp.sum(jnp.where(head == at, two[:, :1], 0.0), axis=0, keepdims=True)
    packed = jnp.concatenate(
        [
            jnp.where(at == 0, zed, one),
            jnp.where(at == 0, one[:, :1], two),
            jnp.broadcast_to(last, (ROWS - 2 * H, F)),
        ],
        axis=0,
    ).astype(bf16)
    for i in range(gb_ref.shape[0]):
        gb_ref[i] = packed


def unfolded(pair_ref, edge_ref, pair, below2, on2):
    folded = pair_ref[pair, 0]
    zero = jnp.zeros_like(folded)
    edge = jnp.broadcast_to(edge_ref[pair], folded.shape).astype(bf16)
    before = jnp.where(below2, folded, jnp.where(on2, edge, zero))
    return before, jnp.where(below2, zero, folded)


def sides_kernel(
    length_ref, q_hbm, g_hbm, p_ref, ds_ref, p0_ref, ds0_ref, da_ref, db_ref, held, sem,
):
    fetch((q_hbm, g_hbm), [held.at[i] for i in range(2)], sem)
    info = position(length_ref)
    row, lane = grids()
    below2, on2 = twice(lane < row), twice(lane == row)

    def run(*refs):
        for pair in range(PAIRS):
            at = pl.ds(pair * F, F)
            q2, g2 = stacked(info, held[0, :, at], held[1, :, at])
            dk = dot(jnp.concatenate(unfolded(ds_ref, ds0_ref, pair, below2, on2), axis=0), q2)
            dv = dot(jnp.concatenate(unfolded(p_ref, p0_ref, pair, below2, on2), axis=0), g2)
            for i, ref in enumerate(refs):
                ref[0, :, at] = dk[i * F : (i + 1) * F].astype(bf16)
                ref[1, :, at] = dv[i * F : (i + 1) * F].astype(bf16)

    @pl.when(info[2] == 1)
    def _():
        run(da_ref, db_ref)

    @pl.when(info[2] == 0)
    def _():
        run(db_ref, da_ref)


def outputs_kernel(
    length_ref, q_hbm, g_hbm, k_hbm, v_hbm, ak_hbm, av_hbm, bk_hbm, bv_hbm,
    p_ref, ds_ref, p0_ref, ds0_ref, fa_ref, fb_ref,
    ctx_ref, dq_ref, gk_ref, gv_ref, held, qg_ref, sem,
):
    info = position(length_ref)
    odd = info[2]
    fetch(
        (q_hbm, g_hbm, k_hbm, v_hbm, ak_hbm, av_hbm, bk_hbm, bv_hbm),
        [qg_ref.at[0], qg_ref.at[1], held.at[1, 0], held.at[1, 1]]
        + [held.at[2 - 2 * odd, i] for i in range(2)]
        + [held.at[2 * odd, i] for i in range(2)],
        sem,
    )
    row, lane = grids()
    below2, on2 = twice(lane < row), twice(lane == row)
    valid = info[0] + row < info[1]
    for pair in range(PAIRS):
        at = pl.ds(pair * F, F)
        q2, g2 = stacked(info, qg_ref[0, :, at], qg_ref[1, :, at])
        p, ds = p_ref[pair, 1], ds_ref[pair, 1]
        for i, (own, out) in enumerate(((dot(ds, q2), gk_ref), (dot(p, g2), gv_ref))):
            total = own + fa_ref[i, :, at].astype(f32) + fb_ref[i, :, at].astype(f32)
            out[:, at] = total.astype(bf16)
        p_before, p_after = unfolded(p_ref, p0_ref, pair, below2, on2)
        ds_before, ds_after = unfolded(ds_ref, ds0_ref, pair, below2, on2)
        keys = jnp.concatenate([held[i, 0, :, at] for i in range(3)], axis=0)
        values = jnp.concatenate([held[i, 1, :, at] for i in range(3)], axis=0)
        ctx_t = dot(jnp.transpose(values), jnp.concatenate([p_before, p, p_after], axis=0))
        dq_t = dot(jnp.transpose(keys), jnp.concatenate([ds_before, ds, ds_after], axis=0))
        ctx = jnp.transpose(jnp.concatenate([ctx_t[:HD, :F], ctx_t[HD:, F:]], axis=0))
        ctx_ref[:, at] = jnp.where(valid, ctx, 0.0).astype(bf16)
        dq = jnp.transpose(jnp.concatenate([dq_t[:HD, :F], dq_t[HD:, F:]], axis=0))
        dq_ref[:, at] = (dq * SCALE).astype(bf16)


def fetch(sources, targets, sem):
    copies = [
        pltpu.make_async_copy(source, target, sem.at[i])
        for i, (source, target) in enumerate(zip(sources, targets))
    ]
    for copy in copies:
        copy.start()
    for copy in copies:
        copy.wait()


def in_vmem(kernel, far, args, out_shape, scratch, flops):
    vmem = pl.BlockSpec(memory_space=pltpu.VMEM)
    hbm = pl.BlockSpec(memory_space=pltpu.HBM)
    return pl.pallas_call(
        kernel,
        in_specs=[pl.BlockSpec(memory_space=pltpu.SMEM)]
        + [hbm] * far
        + [vmem] * (len(args) - 1 - far),
        out_specs=[vmem] * len(out_shape),
        out_shape=out_shape,
        scratch_shapes=scratch,
        compiler_params=pltpu.CompilerParams(vmem_limit_bytes=16 << 20),
        cost_estimate=pl.CostEstimate(flops=flops, bytes_accessed=4 << 20, transcendentals=0),
    )(*args)


def shape(dtype, *dims):
    return jax.ShapeDtypeStruct(dims, dtype)


def own_part(*args):
    return in_vmem(
        own_kernel, 5, args,
        [shape(f32, PAIRS, F, 2 * F)] * 3
        + [shape(f32, PAIRS, 1, 2 * F), shape(bf16, 2, F, D)],
        [
            pltpu.VMEM((3, H, F), f32),
            pltpu.VMEM((H, 2 * W + 1), f32),
            pltpu.VMEM((2, F, D), bf16),
            pltpu.SemaphoreType.DMA((5,)),
        ],
        1 << 30,
    )


def row_part(copies, *args):
    return in_vmem(
        rows_kernel, 0, args,
        [shape(bf16, PAIRS, 2, F, 2 * F)] * 2
        + [shape(f32, PAIRS, 1, 2 * F)] * 2
        + [shape(bf16, copies, ROWS, F)],
        [pltpu.VMEM((2 * H, 8, F), f32)], 1 << 30,
    )


def side_part(*args):
    return in_vmem(
        sides_kernel, 2, args,
        [shape(bf16, 2, F, D)] * 2,
        [pltpu.VMEM((2, F, D), bf16), pltpu.SemaphoreType.DMA((2,))], 1 << 30,
    )


def output_part(*args):
    return in_vmem(
        outputs_kernel, 8, args,
        [shape(bf16, F, D)] * 4,
        [
            pltpu.VMEM((3, 2, F, D), bf16),
            pltpu.VMEM((2, F, D), bf16),
            pltpu.SemaphoreType.DMA((8,)),
        ],
        1 << 30,
    )


def size_of(axes):
    count = 1
    for axis in axes:
        count *= lax.axis_size(axis)
    return count


def step(query_proj, key_proj, value_proj, cotangent, lengths, rel_bias):
    ends = size_of(TM)
    near = [(i, i ^ 1) for i in range(ends)]
    far = [(i, i + 1 if i % 2 else i - 1) for i in range(1, ends - 1)]
    stay = lambda x: pltpu.with_memory_space_constraint(x, pltpu.HBM)
    q, k, v, g = (stay(x[0]) for x in (query_proj, key_proj, value_proj, cotangent))
    table = stay(rel_bias)
    bk = lax.ppermute(key_proj[0], TM, far)
    bv = lax.ppermute(value_proj[0], TM, far)
    ak = lax.ppermute(key_proj[0], TM, near)
    av = lax.ppermute(value_proj[0], TM, near)
    s, gp, bias, edge, qg = own_part(lengths, q, g, k, v, table)
    p, ds, p0, ds0, gb = row_part(
        size_of(Z16), lengths, ak, av, bk, bv, s, gp, bias, edge, qg
    )
    z = lax.all_to_all(gb, Z16, 0, 0, tiled=True)
    da, db = side_part(lengths, q, g, p, ds, p0, ds0)
    fb = lax.ppermute(db, TM, far)
    fa = lax.ppermute(da, TM, near)
    z = jnp.sum(z.astype(f32), axis=0).astype(bf16)
    z = jnp.broadcast_to(z[None], (size_of(XY), ROWS, F))
    z = lax.all_to_all(z, XY, 0, 0, tiled=True)
    ctx, dq, grad_key, grad_value = output_part(
        lengths, q, g, k, v, stay(ak), stay(av), stay(bk), stay(bv), p, ds, p0, ds0, fa, fb
    )
    z = jnp.sum(z.astype(f32), axis=0)
    grad_bias = jnp.concatenate([z[:H], z[H : 2 * H], z[2 * H, :H, None]], axis=1)
    return ctx[None], dq[None], grad_key[None], grad_value[None], grad_bias


def solution(mesh):
    finer = Mesh(mesh.devices.reshape(2, 4, 8, 4, 2), AXES)
    in_specs = (P(DP, TM, None), P(DP, TM, None), P(DP, TM, None), P(DP, TM, None), P(DP), P())
    out_specs = (P(DP, TM, None), P(DP, TM, None), P(DP, TM, None), P(DP, TM, None), P())
    return jax.shard_map(step, mesh=finer, in_specs=in_specs, out_specs=out_specs, check_vma=False)
```

time: 64.8 us -> 66.5 us (1.026)
  starting transfers between devices: 38 us -> 42.7 us
  Pallas kernels: 12.1 us -> 9.45 us
  other arithmetic: 1.67 us -> 0.69 us
    ppermute x4 -> x6, starting transfers between devices: 15 us -> 19 us  [the longest x1 4.92 us: step(): ak = lax.ppermute(key_proj[0], TM, near)]
    all_to_all x1, waiting for transfers between devices: 8.04 us -> 5.61 us  [step(): z = lax.all_to_all(z, XY, 0, 0, tiled=True)]
    all_to_all x1, waiting for transfers between devices: 2.22 us -> 4.59 us  [step(): z = lax.all_to_all(gb, Z16, 0, 0, tiled=True)]
    pallas_call x2 -> x0, Pallas kernels: 1.85 us -> none  [the longest x1 1.04 us: stack(): pl.pallas_call(stack_kernel, in_specs=[pl.BlockSpec(memory_space=pltpu.HB...]
    reduce_sum x1, other arithmetic: 0.93 us -> 0.03 us  [step(): z = jnp.sum(z.astype(f32), axis=0).astype(bf16)]
    pallas_call x3 -> x4, Pallas kernels: 10.3 us -> 9.45 us  [in_vmem(): pl.pallas_call(kernel, in_specs=[pl.BlockSpec(memory_space=pltpu.SMEM)] +...]
  transfers between devices with their start and end apart: 6 -> 8, of which waited for: 2 -> 3; matrix products, arithmetic and copies ran while one was open for 3% -> 1% of each run, Pallas kernels for 12% -> 10%
where the time goes in v3:
time: 66.5 us; the launch traced here: 66 us
  starting transfers between devices  42.7 us (64%)
  waiting for transfers between devices  10.8 us (16%)
  Pallas kernels  9.45 us (14%)
  between operations  1.47 us (2%)
  local copies, waits for them, and re-layouts  0.89 us (1%)
  other arithmetic  0.69 us (1%)
    all_to_all x1, starting transfers between devices, step(): z = lax.all_to_all(gb, Z16, 0, 0, tiled=True)  13.7 us
    all_to_all x1, starting transfers between devices, step(): z = lax.all_to_all(z, XY, 0, 0, tiled=True)  10 us
    pallas_call x4, Pallas kernels, in_vmem(): pl.pallas_call(kernel, in_specs=[pl.BlockSpec(memory_space=pltpu.SMEM)] +...  9.45 us
    all_to_all x1, waiting for transfers between devices, step(): z = lax.all_to_all(z, XY, 0, 0, tiled=True)  5.61 us
    ppermute x1, starting transfers between devices, step(): ak = lax.ppermute(key_proj[0], TM, near)  4.92 us
    all_to_all x1, waiting for transfers between devices, step(): z = lax.all_to_all(gb, Z16, 0, 0, tiled=True)  4.59 us
    ppermute x1, starting transfers between devices, step(): bk = lax.ppermute(key_proj[0], TM, far)  4.5 us
    ppermute x1, starting transfers between devices, step(): fa = lax.ppermute(da, TM, near)  3.82 us
  transfers between devices with their start and end apart: 8, of which 3 were waited for; matrix products, arithmetic and copies ran while one was open for 1% of the time, Pallas kernels for 10%

profile of v3, /device:TPU:1, one launch (start us, length us, event | category | flops | bytes accessed | tf_op | source)
XLA Modules:
  0.0 66.0 jit_solution(3436353848834432591)
XLA Ops:
  0.6 4.5 %collective-permute-start.2 = (bf16[128,768]{1,0:T(8,128)(2,1)}, bf16[128,768]{1,0:T(8,128)(2,1)S(1)}, u32[]{:S(2)}, u32[]{:S(2)}) collective-permute-start(bf16[128,768]{1,0:T(8,128)(2,1)} %bitcast.16), channel_id=1, source_target_pairs={{1,2},{2,1},{3,4},{4,3},{5,6},{6,5},{7,8},{8,7},{9,10},{10,9},{11,... | collective-permute-start | bytes 589832 | tf_op jit(solution)/shard_map/ppermute | solution.py:363
  5.1 4.9 %collective-permute-start = (bf16[128,768]{1,0:T(8,128)(2,1)}, bf16[128,768]{1,0:T(8,128)(2,1)S(1)}, u32[]{:S(2)}, u32[]{:S(2)}) collective-permute-start(bf16[128,768]{1,0:T(8,128)(2,1)} %bitcast.17), channel_id=1, source_target_pairs={{0,1},{1,0},{2,3},{3,2},{4,5},{5,4},{6,7},{7,6},{8,9},{9,8},{10,11... | collective-permute-start | bytes 589832 | tf_op jit(solution)/shard_map/ppermute | solution.py:365
  10.1 1.9 %collective-permute-start.3 = (bf16[128,768]{1,0:T(8,128)(2,1)}, bf16[128,768]{1,0:T(8,128)(2,1)S(1)}, u32[]{:S(2)}, u32[]{:S(2)}) collective-permute-start(bf16[128,768]{1,0:T(8,128)(2,1)} %bitcast.20), channel_id=1, source_target_pairs={{1,2},{2,1},{3,4},{4,3},{5,6},{6,5},{7,8},{8,7},{9,10},{10,9},{11,... | collective-permute-start | bytes 589832 | tf_op jit(solution)/shard_map/ppermute | solution.py:364
  12.0 1.9 %collective-permute-start.1 = (bf16[128,768]{1,0:T(8,128)(2,1)}, bf16[128,768]{1,0:T(8,128)(2,1)S(1)}, u32[]{:S(2)}, u32[]{:S(2)}) collective-permute-start(bf16[128,768]{1,0:T(8,128)(2,1)} %bitcast.21), channel_id=1, source_target_pairs={{0,1},{1,0},{2,3},{3,2},{4,5},{5,4},{6,7},{7,6},{8,9},{9,8},{10,11... | collective-permute-start | bytes 589832 | tf_op jit(solution)/shard_map/ppermute | solution.py:366
  14.6 2.0 %shard_map.101 = (f32[6,128,256]{2,1,0:T(8,128)S(1)}, f32[6,128,256]{2,1,0:T(8,128)S(1)}, f32[6,128,256]{2,1,0:T(8,128)S(1)}, f32[6,1,256]{2,1,0:T(1,128)S(1)}, bf16[2,128,768]{2,1,0:T(8,128)(2,1)S(1)}) custom-call(s32[1]{0:T(128)S(6)} %copy.13.length_ref, bf16[128,768]{1,0:T(8,128)(2,1)} %bitcast.10, bf16[128,768]{1,0:T(8,128)(2,1)} %bitcast.13, ...), custom_call_target="tpu_custom_call" | custom-call | flops 1073741824 | bytes 4194304 | tf_op jit(solution)/shard_map/pallas_call | solution.py:286
  16.6 0.0 collective-permute-done.2.bk_ref.bk_hbm
  16.6 0.0 copy-start
  16.6 0.0 collective-permute-done.ak_ref.ak_hbm
  16.7 0.0 copy-start.1
  16.7 0.6 collective-permute-done.3.bv_ref.bv_hbm
  17.3 0.0 copy-start.2
  17.3 0.0 collective-permute-done.1.av_ref.av_hbm
  17.3 0.0 copy-start.3
  17.3 2.5 %shard_map.102 = (bf16[6,2,128,256]{3,2,1,0:T(8,128)(2,1)S(1)}, bf16[6,2,128,256]{3,2,1,0:T(8,128)(2,1)S(1)}, f32[6,1,256]{2,1,0:T(1,128)S(1)}, f32[6,1,256]{2,1,0:T(1,128)S(1)}, bf16[16,32,128]{2,1,0:T(8,128)(2,1)}) custom-call(s32[1]{0:T(128)S(6)} %copy.13.length_ref, bf16[128,768]{1,0:T(8,128)(2,1)S(1)} %collective-permute-done.ak_ref.ak_hbm, ...), custom_call_target="tpu_custom_call" | custom-call | flops 1073741824 | bytes 4194304 | tf_op jit(solution)/shard_map/pallas_call | solution.py:286
  19.8 0.0 copy-done
  19.8 0.0 copy-done.1
  19.8 0.0 copy-done.2
  19.8 0.0 copy-done.3
  19.8 0.0 copy-start.4
  19.8 13.7 %all-to-all-start = ((bf16[16,32,128]{2,1,0:T(8,128)(2,1)}), bf16[16,32,128]{2,1,0:T(8,128)(2,1)S(1)}, u32[]{:S(2)}, u32[]{:S(2)}) async-start(bf16[16,32,128]{2,1,0:T(8,128)(2,1)} %get-tuple-element.36), calls=%async_computation | async-start | bytes 262144 | tf_op jit(solution)/shard_map/all_to_all | solution.py:371
  33.5 1.6 %shard_map.103 = (bf16[2,128,768]{2,1,0:T(8,128)(2,1)S(1)}, bf16[2,128,768]{2,1,0:T(8,128)(2,1)S(1)}) custom-call(s32[1]{0:T(128)S(6)} %copy.13.length_ref, bf16[128,768]{1,0:T(8,128)(2,1)} %bitcast.11, bf16[128,768]{1,0:T(8,128)(2,1)} %bitcast.14, bf16[6,2,128,256]{3,2,1,0:T(8,128)(2,1)S(1)} %get-tuple-element.26.p_ref, ...), custom_call_target="tpu_custom_call" | custom-call | flops 1073741824 | bytes 4194304 | tf_op jit(solution)/shard_map/pallas_call | solution.py:286
  35.2 0.0 copy-done.4
  35.2 0.0 copy-start.5
  35.2 3.8 %collective-permute-start.4 = (bf16[2,128,768]{2,1,0:T(8,128)(2,1)S(1)}, bf16[2,128,768]{2,1,0:T(8,128)(2,1)S(1)}, u32[]{:S(2)}, u32[]{:S(2)}) collective-permute-start(bf16[2,128,768]{2,1,0:T(8,128)(2,1)S(1)} %get-tuple-element.30), channel_id=1, source_target_pairs={{0,1},{1,0},{2,3},{3,2},{4,5},{5,4},{6,7},{7,6},{8,9},{9,8},{10,11... | collective-permute-start | bytes 1179656 | tf_op jit(solution)/shard_map/ppermute | solution.py:374
  39.0 1.9 %collective-permute-start.5 = (bf16[2,128,768]{2,1,0:T(8,128)(2,1)S(1)}, bf16[2,128,768]{2,1,0:T(8,128)(2,1)S(1)}, u32[]{:S(2)}, u32[]{:S(2)}) collective-permute-start(bf16[2,128,768]{2,1,0:T(8,128)(2,1)S(1)} %get-tuple-element.31), channel_id=1, source_target_pairs={{1,2},{2,1},{3,4},{4,3},{5,6},{6,5},{7,8},{8,7},{9,10},{10,9},{11,... | collective-permute-start | bytes 1179656 | tf_op jit(solution)/shard_map/ppermute | solution.py:373
  40.9 4.6 %all-to-all-done = bf16[16,32,128]{2,1,0:T(8,128)(2,1)S(1)} async-done(((bf16[16,32,128]{2,1,0:T(8,128)(2,1)}), bf16[16,32,128]{2,1,0:T(8,128)(2,1)S(1)}, u32[]{:S(2)}, u32[]{:S(2)}) %all-to-all-start) | async-done | bytes 131104 | tf_op jit(solution)/shard_map/all_to_all | solution.py:371
  45.5 0.8 %broadcast_in_dim.22 = bf16[32,32,128]{2,1,0:T(8,128)(2,1)} broadcast(bf16[32,128]{1,0:T(8,128)(2,1)S(1)} %reduce_sum.21), dimensions={1,2} | broadcast | bytes 270336 | tf_op jit(solution)/shard_map/broadcast_in_dim | solution.py:376
  46.3 10.0 %all-to-all-start.1 = ((bf16[32,32,128]{2,1,0:T(8,128)(2,1)}), bf16[32,32,128]{2,1,0:T(8,128)(2,1)S(1)}, u32[]{:S(2)}, u32[]{:S(2)}) async-start(bf16[32,32,128]{2,1,0:T(8,128)(2,1)} %broadcast_in_dim.22), calls=%async_computation.1 | async-start | bytes 524288 | tf_op jit(solution)/shard_map/all_to_all | solution.py:377
  56.3 0.0 collective-permute-done.4.fa_ref
  56.3 0.0 collective-permute-done.5.fb_ref
  56.3 0.0 copy-done.5
  56.3 3.2 %shard_map.104 = (bf16[128,768]{1,0:T(8,128)(2,1)}, bf16[128,768]{1,0:T(8,128)(2,1)}, bf16[128,768]{1,0:T(8,128)(2,1)}, bf16[128,768]{1,0:T(8,128)(2,1)}) custom-call(s32[1]{0:T(128)S(6)} %copy.13.length_ref, bf16[128,768]{1,0:T(8,128)(2,1)} %bitcast.12, bf16[128,768]{1,0:T(8,128)(2,1)} %bitcast.15, bf16[128,768]{1,0:T(8,128)(2,1)} %bitcast.19, ...), custom_call_target="tpu_custom_call" | custom-call | flops 1073741824 | bytes 4194304 | tf_op jit(solution)/shard_map/pallas_call | solution.py:286
  59.6 5.6 %all-to-all-done.1 = bf16[32,32,128]{2,1,0:T(8,128)(2,1)S(1)} async-done(((bf16[32,32,128]{2,1,0:T(8,128)(2,1)}), bf16[32,32,128]{2,1,0:T(8,128)(2,1)S(1)}, u32[]{:S(2)}, u32[]{:S(2)}) %all-to-all-start.1) | async-done | bytes 262176 | tf_op jit(solution)/shard_map/all_to_all | solution.py:377
  65.3 0.1 copy.12
  65.4 0.6 pad_maximum_fusion
  (4 shorter events, 0.1 us)
Async XLA Ops:
  0.6 16.0 %collective-permute-start.2 = (bf16[128,768]{1,0:T(8,128)(2,1)}, bf16[128,768]{1,0:T(8,128)(2,1)S(1)}, u32[]{:S(2)}, u32[]{:S(2)}) collective-permute-start(bf16[128,768]{1,0:T(8,128)(2,1)} %bitcast.16), channel_id=1, source_target_pairs={{1,2},{2,1},{3,4},{4,3},{5,6},{6,5},{7,8},{8,7},{9,10},{10,9},{11,... | collective-permute-start | bytes 589832 | tf_op jit(solution)/shard_map/ppermute | solution.py:363
  5.1 11.5 %collective-permute-start = (bf16[128,768]{1,0:T(8,128)(2,1)}, bf16[128,768]{1,0:T(8,128)(2,1)S(1)}, u32[]{:S(2)}, u32[]{:S(2)}) collective-permute-start(bf16[128,768]{1,0:T(8,128)(2,1)} %bitcast.17), channel_id=1, source_target_pairs={{0,1},{1,0},{2,3},{3,2},{4,5},{5,4},{6,7},{7,6},{8,9},{9,8},{10,11... | collective-permute-start | bytes 589832 | tf_op jit(solution)/shard_map/ppermute | solution.py:365
  10.1 7.2 %collective-permute-start.3 = (bf16[128,768]{1,0:T(8,128)(2,1)}, bf16[128,768]{1,0:T(8,128)(2,1)S(1)}, u32[]{:S(2)}, u32[]{:S(2)}) collective-permute-start(bf16[128,768]{1,0:T(8,128)(2,1)} %bitcast.20), channel_id=1, source_target_pairs={{1,2},{2,1},{3,4},{4,3},{5,6},{6,5},{7,8},{8,7},{9,10},{10,9},{11,... | collective-permute-start | bytes 589832 | tf_op jit(solution)/shard_map/ppermute | solution.py:364
  12.0 5.3 %collective-permute-start.1 = (bf16[128,768]{1,0:T(8,128)(2,1)}, bf16[128,768]{1,0:T(8,128)(2,1)S(1)}, u32[]{:S(2)}, u32[]{:S(2)}) collective-permute-start(bf16[128,768]{1,0:T(8,128)(2,1)} %bitcast.21), channel_id=1, source_target_pairs={{0,1},{1,0},{2,3},{3,2},{4,5},{5,4},{6,7},{7,6},{8,9},{9,8},{10,11... | collective-permute-start | bytes 589832 | tf_op jit(solution)/shard_map/ppermute | solution.py:366
  16.6 3.2 %copy-start = (bf16[128,768]{1,0:T(8,128)(2,1)}, bf16[128,768]{1,0:T(8,128)(2,1)S(1)}, u32[]{:S(2)}) copy-start(bf16[128,768]{1,0:T(8,128)(2,1)S(1)} %collective-permute-done.2.bk_ref.bk_hbm) | copy-start | bytes 589828
  16.7 3.2 %copy-start.1 = (bf16[128,768]{1,0:T(8,128)(2,1)}, bf16[128,768]{1,0:T(8,128)(2,1)S(1)}, u32[]{:S(2)}) copy-start(bf16[128,768]{1,0:T(8,128)(2,1)S(1)} %collective-permute-done.ak_ref.ak_hbm) | copy-start | bytes 589828
  17.3 2.5 %copy-start.2 = (bf16[128,768]{1,0:T(8,128)(2,1)}, bf16[128,768]{1,0:T(8,128)(2,1)S(1)}, u32[]{:S(2)}) copy-start(bf16[128,768]{1,0:T(8,128)(2,1)S(1)} %collective-permute-done.3.bv_ref.bv_hbm) | copy-start | bytes 589828
  17.3 2.5 %copy-start.3 = (bf16[128,768]{1,0:T(8,128)(2,1)}, bf16[128,768]{1,0:T(8,128)(2,1)S(1)}, u32[]{:S(2)}) copy-start(bf16[128,768]{1,0:T(8,128)(2,1)S(1)} %collective-permute-done.1.av_ref.av_hbm) | copy-start | bytes 589828
  19.8 15.3 %copy-start.4 = (bf16[6,2,128,256]{3,2,1,0:T(8,128)(2,1)}, bf16[6,2,128,256]{3,2,1,0:T(8,128)(2,1)S(1)}, u32[]{:S(2)}) copy-start(bf16[6,2,128,256]{3,2,1,0:T(8,128)(2,1)S(1)} %get-tuple-element.27.ds_ref) | copy-start | bytes 2359300
  19.8 25.7 %all-to-all-start = ((bf16[16,32,128]{2,1,0:T(8,128)(2,1)}), bf16[16,32,128]{2,1,0:T(8,128)(2,1)S(1)}, u32[]{:S(2)}, u32[]{:S(2)}) async-start(bf16[16,32,128]{2,1,0:T(8,128)(2,1)} %get-tuple-element.36), calls=%async_computation | async-start | bytes 262144 | tf_op jit(solution)/shard_map/all_to_all | solution.py:371
  35.2 21.2 %copy-start.5 = (bf16[6,2,128,256]{3,2,1,0:T(8,128)(2,1)S(1)}, bf16[6,2,128,256]{3,2,1,0:T(8,128)(2,1)}, u32[]{:S(2)}) copy-start(bf16[6,2,128,256]{3,2,1,0:T(8,128)(2,1)} %copy-done.4) | copy-start | bytes 2359300
  35.2 21.1 %collective-permute-start.4 = (bf16[2,128,768]{2,1,0:T(8,128)(2,1)S(1)}, bf16[2,128,768]{2,1,0:T(8,128)(2,1)S(1)}, u32[]{:S(2)}, u32[]{:S(2)}) collective-permute-start(bf16[2,128,768]{2,1,0:T(8,128)(2,1)S(1)} %get-tuple-element.30), channel_id=1, source_target_pairs={{0,1},{1,0},{2,3},{3,2},{4,5},{5,4},{6,7},{7,6},{8,9},{9,8},{10,11... | collective-permute-start | bytes 1179656 | tf_op jit(solution)/shard_map/ppermute | solution.py:374
  39.0 17.3 %collective-permute-start.5 = (bf16[2,128,768]{2,1,0:T(8,128)(2,1)S(1)}, bf16[2,128,768]{2,1,0:T(8,128)(2,1)S(1)}, u32[]{:S(2)}, u32[]{:S(2)}) collective-permute-start(bf16[2,128,768]{2,1,0:T(8,128)(2,1)S(1)} %get-tuple-element.31), channel_id=1, source_target_pairs={{1,2},{2,1},{3,4},{4,3},{5,6},{6,5},{7,8},{8,7},{9,10},{10,9},{11,... | collective-permute-start | bytes 1179656 | tf_op jit(solution)/shard_map/ppermute | solution.py:373
  46.3 18.9 %all-to-all-start.1 = ((bf16[32,32,128]{2,1,0:T(8,128)(2,1)}), bf16[32,32,128]{2,1,0:T(8,128)(2,1)S(1)}, u32[]{:S(2)}, u32[]{:S(2)}) async-start(bf16[32,32,128]{2,1,0:T(8,128)(2,1)} %broadcast_in_dim.22), calls=%async_computation.1 | async-start | bytes 524288 | tf_op jit(solution)/shard_map/all_to_all | solution.py:377

commit v4 on v3

--- a/solution.py
+++ b/solution.py
@@ -74,14 +74,10 @@
 
 
 def own_kernel(
-    length_ref, q_hbm, g_hbm, k_hbm, v_hbm, table_hbm,
-    s_ref, gp_ref, bias_ref, edge_ref, qg_ref, rt_ref, table_ref, kv_ref, sem,
+    length_ref, q_hbm, g_hbm, table_hbm, kv_ref,
+    s_ref, gp_ref, bias_ref, edge_ref, q2_ref, g2_ref, rt_ref, table_ref, qg_ref, sem,
 ):
-    fetch(
-        (q_hbm, g_hbm, k_hbm, v_hbm, table_hbm),
-        (qg_ref.at[0], qg_ref.at[1], kv_ref.at[0], kv_ref.at[1], table_ref),
-        sem,
-    )
+    fetch((q_hbm, g_hbm, table_hbm), (qg_ref.at[0], qg_ref.at[1], table_ref), sem)
     info = position(length_ref)
     first, length = info[0], info[1]
     row, lane = grids()
@@ -100,6 +96,7 @@
     def step(pair, carry):
         at = lanes(pair)
         q2, g2 = stacked(info, qg_ref[0, :, at], qg_ref[1, :, at])
+        q2_ref[pair], g2_ref[pair] = q2, g2
         own, other, ends = [], [], []
         for h in range(2):
             line = lambda which: rt_ref[which, pl.ds(2 * pair + h, 1), :]
@@ -119,35 +116,38 @@
 
 
 def rows_kernel(
-    length_ref, ak_ref, av_ref, bk_ref, bv_ref, s_ref, gp_ref, bias_ref, edge_ref, qg_ref,
+    length_ref, a_ref, b_ref, s_ref, gp_ref, bias_ref, edge_ref, q2_ref, g2_ref,
     p_ref, ds_ref, p0_ref, ds0_ref, gb_ref, acc_ref,
 ):
     info = position(length_ref)
     row, lane = grids()
     below, on = lane < row, lane == row
     below2, on2 = twice(below), twice(on)
-
-    def run(before_refs, after_refs):
+    hit = twice(lane & 7 == row)[:8]
+
+    def run(before_ref, after_ref):
         for pair in range(PAIRS):
             at = pl.ds(pair * F, F)
-            q2, g2 = stacked(info, qg_ref[0, :, at], qg_ref[1, :, at])
 
             def around(which, rows2):
-                left = dot(before_refs[which][:, at], rows2, NT)
-                right = dot(after_refs[which][:, at], rows2, NT)
-                edge = jnp.sum(jnp.where(on2, left, 0.0), axis=0, keepdims=True)
+                left = dot(before_ref[which, :, at], rows2, NT)
+                right = dot(after_ref[which, :, at], rows2, NT)
+                edge = jnp.zeros((8, 2 * F), f32)
+                for k in range(16):
+                    edge = jnp.where(on2[8 * k : 8 * k + 8], left[8 * k : 8 * k + 8], edge)
+                edge = jnp.sum(jnp.where(hit, edge, 0.0), axis=0, keepdims=True)
                 return jnp.where(below2, left, right), edge
 
-            s1, s0 = around(0, q2)
+            s1, s0 = around(0, q2_ref[pair])
             s1, s0, s2 = s1 + bias_ref[pair], s0 + edge_ref[pair], s_ref[pair]
             top = jnp.maximum(jnp.max(jnp.maximum(s1, s2), axis=0, keepdims=True), s0)
             e0, e1, e2 = jnp.exp(s0 - top), jnp.exp(s1 - top), jnp.exp(s2 - top)
+            g1, g0 = around(1, g2_ref[pair])
+            g2 = gp_ref[pair]
             inverse = 1.0 / (e0 + jnp.sum(e1 + e2, axis=0, keepdims=True))
+            delta = (e0 * g0 + jnp.sum(e1 * g1 + e2 * g2, axis=0, keepdims=True)) * inverse
             p0, p1, p2 = e0 * inverse, e1 * inverse, e2 * inverse
-            g1, g0 = around(1, g2)
-            g2_own = gp_ref[pair]
-            delta = p0 * g0 + jnp.sum(p1 * g1 + p2 * g2_own, axis=0, keepdims=True)
-            d0, d1, d2 = p0 * (g0 - delta), p1 * (g1 - delta), p2 * (g2_own - delta)
+            d0, d1, d2 = p0 * (g0 - delta), p1 * (g1 - delta), p2 * (g2 - delta)
             p_ref[pair, 0], p_ref[pair, 1] = p1.astype(bf16), p2.astype(bf16)
             ds_ref[pair, 0], ds_ref[pair, 1] = d1.astype(bf16), d2.astype(bf16)
             p0_ref[pair], ds0_ref[pair] = p0, d0
@@ -163,11 +163,11 @@
 
     @pl.when(info[2] == 1)
     def _():
-        run((ak_ref, av_ref), (bk_ref, bv_ref))
+        run(a_ref, b_ref)
 
     @pl.when(info[2] == 0)
     def _():
-        run((bk_ref, bv_ref), (ak_ref, av_ref))
+        run(b_ref, a_ref)
 
     summed = acc_ref[:, 0, :]
     for s in range(1, 8):
@@ -234,17 +234,16 @@
 
 
 def outputs_kernel(
-    length_ref, q_hbm, g_hbm, k_hbm, v_hbm, ak_hbm, av_hbm, bk_hbm, bv_hbm,
+    length_ref, q_hbm, g_hbm, k_hbm, v_hbm, a_hbm, b_hbm,
     p_ref, ds_ref, p0_ref, ds0_ref, fa_ref, fb_ref,
     ctx_ref, dq_ref, gk_ref, gv_ref, held, qg_ref, sem,
 ):
     info = position(length_ref)
     odd = info[2]
     fetch(
-        (q_hbm, g_hbm, k_hbm, v_hbm, ak_hbm, av_hbm, bk_hbm, bv_hbm),
+        (q_hbm, g_hbm, k_hbm, v_hbm, a_hbm, b_hbm),
         [qg_ref.at[0], qg_ref.at[1], held.at[1, 0], held.at[1, 1]]
-        + [held.at[2 - 2 * odd, i] for i in range(2)]
-        + [held.at[2 * odd, i] for i in range(2)],
+        + [held.at[2 - 2 * odd], held.at[2 * odd]],
         sem,
     )
     row, lane = grids()
@@ -280,6 +279,22 @@
         copy.wait()
 
 
+def stack_kernel(k_hbm, v_hbm, out_ref, sem):
+    fetch((k_hbm, v_hbm), (out_ref.at[0], out_ref.at[1]), sem)
+
+
+def stack(k, v):
+    return pl.pallas_call(
+        stack_kernel,
+        in_specs=[pl.BlockSpec(memory_space=pltpu.HBM)] * 2,
+        out_specs=pl.BlockSpec(memory_space=pltpu.VMEM),
+        out_shape=shape(bf16, 2, F, D),
+        scratch_shapes=[pltpu.SemaphoreType.DMA((2,))],
+        compiler_params=pltpu.CompilerParams(vmem_limit_bytes=1 << 20),
+        name="stack",
+    )(k, v)
+
+
 def in_vmem(kernel, far, args, out_shape, scratch, flops):
     vmem = pl.BlockSpec(memory_space=pltpu.VMEM)
     hbm = pl.BlockSpec(memory_space=pltpu.HBM)
@@ -302,14 +317,15 @@
 
 def own_part(*args):
     return in_vmem(
-        own_kernel, 5, args,
+        own_kernel, 3, args,
         [shape(f32, PAIRS, F, 2 * F)] * 3
-        + [shape(f32, PAIRS, 1, 2 * F), shape(bf16, 2, F, D)],
+        + [shape(f32, PAIRS, 1, 2 * F)]
+        + [shape(bf16, PAIRS, 2 * F, F)] * 2,
         [
             pltpu.VMEM((3, H, F), f32),
             pltpu.VMEM((H, 2 * W + 1), f32),
             pltpu.VMEM((2, F, D), bf16),
-            pltpu.SemaphoreType.DMA((5,)),
+            pltpu.SemaphoreType.DMA((3,)),
         ],
         1 << 30,
     )
@@ -335,12 +351,12 @@
 
 def output_part(*args):
     return in_vmem(
-        outputs_kernel, 8, args,
+        outputs_kernel, 6, args,
         [shape(bf16, F, D)] * 4,
         [
             pltpu.VMEM((3, 2, F, D), bf16),
             pltpu.VMEM((2, F, D), bf16),
-            pltpu.SemaphoreType.DMA((8,)),
+            pltpu.SemaphoreType.DMA((6,)),
         ],
         1 << 30,
     )
@@ -360,23 +376,20 @@
     stay = lambda x: pltpu.with_memory_space_constraint(x, pltpu.HBM)
     q, k, v, g = (stay(x[0]) for x in (query_proj, key_proj, value_proj, cotangent))
     table = stay(rel_bias)
-    bk = lax.ppermute(key_proj[0], TM, far)
-    bv = lax.ppermute(value_proj[0], TM, far)
-    ak = lax.ppermute(key_proj[0], TM, near)
-    av = lax.ppermute(value_proj[0], TM, near)
-    s, gp, bias, edge, qg = own_part(lengths, q, g, k, v, table)
-    p, ds, p0, ds0, gb = row_part(
-        size_of(Z16), lengths, ak, av, bk, bv, s, gp, bias, edge, qg
-    )
-    z = lax.all_to_all(gb, Z16, 0, 0, tiled=True)
+    kv = stack(k, v)
+    side_b = lax.ppermute(kv, TM, far)
+    side_a = lax.ppermute(kv, TM, near)
+    s, gp, bias, edge, q2, g2 = own_part(lengths, q, g, table, kv)
+    p, ds, p0, ds0, gb = row_part(size_of(XY), lengths, side_a, side_b, s, gp, bias, edge, q2, g2)
+    z = lax.all_to_all(gb, XY, 0, 0, tiled=True)
     da, db = side_part(lengths, q, g, p, ds, p0, ds0)
     fb = lax.ppermute(db, TM, far)
     fa = lax.ppermute(da, TM, near)
     z = jnp.sum(z.astype(f32), axis=0).astype(bf16)
-    z = jnp.broadcast_to(z[None], (size_of(XY), ROWS, F))
-    z = lax.all_to_all(z, XY, 0, 0, tiled=True)
+    z = jnp.broadcast_to(z[None], (size_of(Z16), ROWS, F))
+    z = lax.all_to_all(z, Z16, 0, 0, tiled=True)
     ctx, dq, grad_key, grad_value = output_part(
-        lengths, q, g, k, v, stay(ak), stay(av), stay(bk), stay(bv), p, ds, p0, ds0, fa, fb
+        lengths, q, g, k, v, stay(side_a), stay(side_b), p, ds, p0, ds0, fa, fb
     )
     z = jnp.sum(z.astype(f32), axis=0)
     grad_bias = jnp.concatenate([z[:H], z[H : 2 * H], z[2 * H, :H, None]], axis=1)

time: 66.5 us -> 62.1 us (0.934)
  the two profiles are of different devices: /device:TPU:1 before, /device:TPU:32 now
where the time goes in v4:
time: 62.1 us; the launch traced here: 61.7 us
  starting transfers between devices  33.7 us (54%)
  waiting for transfers between devices  14.9 us (24%)
  Pallas kernels  10.2 us (16%)
  between operations  1.38 us (2%)
  local copies, waits for them, and re-layouts  0.78 us (1%)
  other arithmetic  0.69 us (1%)
    all_to_all x1, starting transfers between devices, step(): z = lax.all_to_all(z, Z16, 0, 0, tiled=True)  15.2 us
    all_to_all x1, waiting for transfers between devices, step(): z = lax.all_to_all(z, Z16, 0, 0, tiled=True)  11.1 us
    pallas_call x4, Pallas kernels, in_vmem(): pl.pallas_call(kernel, in_specs=[pl.BlockSpec(memory_space=pltpu.SMEM)] +...  9.17 us
    all_to_all x1, starting transfers between devices, step(): z = lax.all_to_all(gb, XY, 0, 0, tiled=True)  6.49 us
    ppermute x1, starting transfers between devices, step(): fb = lax.ppermute(db, TM, far)  4.29 us
    ppermute x1, starting transfers between devices, step(): side_b = lax.ppermute(kv, TM, far)  3.65 us
    ppermute x1, waiting for transfers between devices, step(): side_b = lax.ppermute(kv, TM, far)  3.09 us
    ppermute x1, starting transfers between devices, step(): fa = lax.ppermute(da, TM, near)  2.18 us
  transfers between devices with their start and end apart: 6, of which 3 were waited for; matrix products, arithmetic and copies ran while one was open for 1% of the time, Pallas kernels for 11%

profile of v4, /device:TPU:32, one launch (start us, length us, event | category | flops | bytes accessed | tf_op | source)
XLA Modules:
  0.0 61.7 jit_solution(2396861906165141216)
XLA Ops:
  0.6 1.0 %stack.1.kv_ref = bf16[2,128,768]{2,1,0:T(8,128)(2,1)S(1)} custom-call(bf16[128,768]{1,0:T(8,128)(2,1)} %bitcast.10, bf16[128,768]{1,0:T(8,128)(2,1)} %bitcast.12), custom_call_target="tpu_custom_call" | custom-call | tf_op jit(solution)/shard_map/stack/pallas_call | solution.py:287
  1.7 3.7 %collective-permute-start.1 = (bf16[2,128,768]{2,1,0:T(8,128)(2,1)S(1)}, bf16[2,128,768]{2,1,0:T(8,128)(2,1)S(1)}, u32[]{:S(2)}, u32[]{:S(2)}) collective-permute-start(bf16[2,128,768]{2,1,0:T(8,128)(2,1)S(1)} %stack.1.kv_ref), channel_id=1, source_target_pairs={{1,2},{2,1},{3,4},{4,3},{5,6},{6,5},{7,8},{8,7},{9,10},{10,9},{11,... | collective-permute-start | bytes 1179656 | tf_op jit(solution)/shard_map/ppermute | solution.py:380
  5.3 1.9 %collective-permute-start = (bf16[2,128,768]{2,1,0:T(8,128)(2,1)S(1)}, bf16[2,128,768]{2,1,0:T(8,128)(2,1)S(1)}, u32[]{:S(2)}, u32[]{:S(2)}) collective-permute-start(bf16[2,128,768]{2,1,0:T(8,128)(2,1)S(1)} %stack.1.kv_ref), channel_id=1, source_target_pairs={{0,1},{1,0},{2,3},{3,2},{4,5},{5,4},{6,7},{7,6},{8,9},{9,8},{10,11... | collective-permute-start | bytes 1179656 | tf_op jit(solution)/shard_map/ppermute | solution.py:381
  7.9 1.9 %shard_map.101 = (f32[6,128,256]{2,1,0:T(8,128)S(1)}, f32[6,128,256]{2,1,0:T(8,128)S(1)}, f32[6,128,256]{2,1,0:T(8,128)S(1)}, f32[6,1,256]{2,1,0:T(1,128)S(1)}, ...) custom-call(s32[1]{0:T(128)S(6)} %copy.13.length_ref, bf16[128,768]{1,0:T(8,128)(2,1)} %bitcast.14, ...), custom_call_target="tpu_custom_call" | custom-call | flops 1073741824 | bytes 4194304 | tf_op jit(solution)/shard_map/pallas_call | solution.py:301
  9.8 3.1 %collective-permute-done.1.b_ref.b_hbm = bf16[2,128,768]{2,1,0:T(8,128)(2,1)S(1)} collective-permute-done((bf16[2,128,768]{2,1,0:T(8,128)(2,1)S(1)}, bf16[2,128,768]{2,1,0:T(8,128)(2,1)S(1)}, u32[]{:S(2)}, u32[]{:S(2)}) %collective-permute-start.1) | collective-permute-done | bytes 393248 | tf_op jit(solution)/shard_map/ppermute | solution.py:380
  12.9 0.0 copy-start
  12.9 0.0 collective-permute-done.a_ref.a_hbm
  12.9 0.0 copy-start.1
  12.9 2.4 %shard_map.102 = (bf16[6,2,128,256]{3,2,1,0:T(8,128)(2,1)S(1)}, bf16[6,2,128,256]{3,2,1,0:T(8,128)(2,1)S(1)}, f32[6,1,256]{2,1,0:T(1,128)S(1)}, f32[6,1,256]{2,1,0:T(1,128)S(1)}, bf16[32,32,128]{2,1,0:T(8,128)(2,1)}) custom-call(s32[1]{0:T(128)S(6)} %copy.13.length_ref, bf16[2,128,768]{2,1,0:T(8,128)(2,1)S(1)} %collective-permute-done.a_ref.a_hbm, ...), custom_call_target="tpu_custom_call" | custom-call | flops 1073741824 | bytes 4194304 | tf_op jit(solution)/shard_map/pallas_call | solution.py:301
  15.3 0.0 copy-done
  15.3 0.0 copy-done.1
  15.3 6.5 %all-to-all-start = ((bf16[32,32,128]{2,1,0:T(8,128)(2,1)}), bf16[32,32,128]{2,1,0:T(8,128)(2,1)S(1)}, u32[]{:S(2)}, u32[]{:S(2)}) async-start(bf16[32,32,128]{2,1,0:T(8,128)(2,1)} %get-tuple-element.38), calls=%async_computation | async-start | bytes 524288 | tf_op jit(solution)/shard_map/all_to_all | solution.py:384
  21.8 1.6 %shard_map.103 = (bf16[2,128,768]{2,1,0:T(8,128)(2,1)S(1)}, bf16[2,128,768]{2,1,0:T(8,128)(2,1)S(1)}) custom-call(s32[1]{0:T(128)S(6)} %copy.13.length_ref, bf16[128,768]{1,0:T(8,128)(2,1)} %bitcast.15, bf16[128,768]{1,0:T(8,128)(2,1)} %bitcast.18, bf16[6,2,128,256]{3,2,1,0:T(8,128)(2,1)S(1)} %get-tuple-element.28.p_ref, ...), custom_call_target="tpu_custom_call" | custom-call | flops 1073741824 | bytes 4194304 | tf_op jit(solution)/shard_map/pallas_call | solution.py:301
  23.5 2.2 %collective-permute-start.2 = (bf16[2,128,768]{2,1,0:T(8,128)(2,1)S(1)}, bf16[2,128,768]{2,1,0:T(8,128)(2,1)S(1)}, u32[]{:S(2)}, u32[]{:S(2)}) collective-permute-start(bf16[2,128,768]{2,1,0:T(8,128)(2,1)S(1)} %get-tuple-element.32), channel_id=1, source_target_pairs={{0,1},{1,0},{2,3},{3,2},{4,5},{5,4},{6,7},{7,6},{8,9},{9,8},{10,11... | collective-permute-start | bytes 1179656 | tf_op jit(solution)/shard_map/ppermute | solution.py:387
  25.7 4.3 %collective-permute-start.3 = (bf16[2,128,768]{2,1,0:T(8,128)(2,1)S(1)}, bf16[2,128,768]{2,1,0:T(8,128)(2,1)S(1)}, u32[]{:S(2)}, u32[]{:S(2)}) collective-permute-start(bf16[2,128,768]{2,1,0:T(8,128)(2,1)S(1)} %get-tuple-element.33), channel_id=1, source_target_pairs={{1,2},{2,1},{3,4},{4,3},{5,6},{6,5},{7,8},{8,7},{9,10},{10,9},{11,... | collective-permute-start | bytes 1179656 | tf_op jit(solution)/shard_map/ppermute | solution.py:386
  30.0 0.6 %all-to-all-done = bf16[32,32,128]{2,1,0:T(8,128)(2,1)S(1)} async-done(((bf16[32,32,128]{2,1,0:T(8,128)(2,1)}), bf16[32,32,128]{2,1,0:T(8,128)(2,1)S(1)}, u32[]{:S(2)}, u32[]{:S(2)}) %all-to-all-start) | async-done | bytes 262176 | tf_op jit(solution)/shard_map/all_to_all | solution.py:384
  30.6 0.1 reduce_sum.21
  30.7 0.7 %broadcast_in_dim.22 = bf16[16,32,128]{2,1,0:T(8,128)(2,1)} broadcast(bf16[32,128]{1,0:T(8,128)(2,1)S(1)} %reduce_sum.21), dimensions={1,2} | broadcast | bytes 139264 | tf_op jit(solution)/shard_map/broadcast_in_dim | solution.py:389
  31.3 15.2 %all-to-all-start.1 = ((bf16[16,32,128]{2,1,0:T(8,128)(2,1)}), bf16[16,32,128]{2,1,0:T(8,128)(2,1)S(1)}, u32[]{:S(2)}, u32[]{:S(2)}) async-start(bf16[16,32,128]{2,1,0:T(8,128)(2,1)} %broadcast_in_dim.22), calls=%async_computation.1 | async-start | bytes 262144 | tf_op jit(solution)/shard_map/all_to_all | solution.py:390
  46.6 0.0 collective-permute-done.2.fa_ref
  46.6 0.0 collective-permute-done.3.fb_ref
  46.6 3.2 %shard_map.104 = (bf16[128,768]{1,0:T(8,128)(2,1)}, bf16[128,768]{1,0:T(8,128)(2,1)}, bf16[128,768]{1,0:T(8,128)(2,1)}, bf16[128,768]{1,0:T(8,128)(2,1)}) custom-call(s32[1]{0:T(128)S(6)} %copy.13.length_ref, bf16[128,768]{1,0:T(8,128)(2,1)} %bitcast.16, bf16[128,768]{1,0:T(8,128)(2,1)} %bitcast.19, bf16[128,768]{1,0:T(8,128)(2,1)} %bitcast.11, ...), custom_call_target="tpu_custom_call" | custom-call | flops 1073741824 | bytes 4194304 | tf_op jit(solution)/shard_map/pallas_call | solution.py:301
  49.8 11.1 %all-to-all-done.1 = bf16[16,32,128]{2,1,0:T(8,128)(2,1)S(1)} async-done(((bf16[16,32,128]{2,1,0:T(8,128)(2,1)}), bf16[16,32,128]{2,1,0:T(8,128)(2,1)S(1)}, u32[]{:S(2)}, u32[]{:S(2)}) %all-to-all-start.1) | async-done | bytes 131104 | tf_op jit(solution)/shard_map/all_to_all | solution.py:390
  61.0 0.1 copy.12
  61.1 0.6 pad_maximum_fusion
  (3 shorter events, 0.0 us)
Async XLA Ops:
  1.7 11.2 %collective-permute-start.1 = (bf16[2,128,768]{2,1,0:T(8,128)(2,1)S(1)}, bf16[2,128,768]{2,1,0:T(8,128)(2,1)S(1)}, u32[]{:S(2)}, u32[]{:S(2)}) collective-permute-start(bf16[2,128,768]{2,1,0:T(8,128)(2,1)S(1)} %stack.1.kv_ref), channel_id=1, source_target_pairs={{1,2},{2,1},{3,4},{4,3},{5,6},{6,5},{7,8},{8,7},{9,10},{10,9},{11,... | collective-permute-start | bytes 1179656 | tf_op jit(solution)/shard_map/ppermute | solution.py:380
  5.3 7.6 %collective-permute-start = (bf16[2,128,768]{2,1,0:T(8,128)(2,1)S(1)}, bf16[2,128,768]{2,1,0:T(8,128)(2,1)S(1)}, u32[]{:S(2)}, u32[]{:S(2)}) collective-permute-start(bf16[2,128,768]{2,1,0:T(8,128)(2,1)S(1)} %stack.1.kv_ref), channel_id=1, source_target_pairs={{0,1},{1,0},{2,3},{3,2},{4,5},{5,4},{6,7},{7,6},{8,9},{9,8},{10,11... | collective-permute-start | bytes 1179656 | tf_op jit(solution)/shard_map/ppermute | solution.py:381
  12.9 2.4 %copy-start = (bf16[2,128,768]{2,1,0:T(8,128)(2,1)}, bf16[2,128,768]{2,1,0:T(8,128)(2,1)S(1)}, u32[]{:S(2)}) copy-start(bf16[2,128,768]{2,1,0:T(8,128)(2,1)S(1)} %collective-permute-done.1.b_ref.b_hbm) | copy-start | bytes 1179652
  12.9 2.4 %copy-start.1 = (bf16[2,128,768]{2,1,0:T(8,128)(2,1)}, bf16[2,128,768]{2,1,0:T(8,128)(2,1)S(1)}, u32[]{:S(2)}) copy-start(bf16[2,128,768]{2,1,0:T(8,128)(2,1)S(1)} %collective-permute-done.a_ref.a_hbm) | copy-start | bytes 1179652
  15.3 15.3 %all-to-all-start = ((bf16[32,32,128]{2,1,0:T(8,128)(2,1)}), bf16[32,32,128]{2,1,0:T(8,128)(2,1)S(1)}, u32[]{:S(2)}, u32[]{:S(2)}) async-start(bf16[32,32,128]{2,1,0:T(8,128)(2,1)} %get-tuple-element.38), calls=%async_computation | async-start | bytes 524288 | tf_op jit(solution)/shard_map/all_to_all | solution.py:384
  23.5 23.1 %collective-permute-start.2 = (bf16[2,128,768]{2,1,0:T(8,128)(2,1)S(1)}, bf16[2,128,768]{2,1,0:T(8,128)(2,1)S(1)}, u32[]{:S(2)}, u32[]{:S(2)}) collective-permute-start(bf16[2,128,768]{2,1,0:T(8,128)(2,1)S(1)} %get-tuple-element.32), channel_id=1, source_target_pairs={{0,1},{1,0},{2,3},{3,2},{4,5},{5,4},{6,7},{7,6},{8,9},{9,8},{10,11... | collective-permute-start | bytes 1179656 | tf_op jit(solution)/shard_map/ppermute | solution.py:387
  25.7 20.9 %collective-permute-start.3 = (bf16[2,128,768]{2,1,0:T(8,128)(2,1)S(1)}, bf16[2,128,768]{2,1,0:T(8,128)(2,1)S(1)}, u32[]{:S(2)}, u32[]{:S(2)}) collective-permute-start(bf16[2,128,768]{2,1,0:T(8,128)(2,1)S(1)} %get-tuple-element.33), channel_id=1, source_target_pairs={{1,2},{2,1},{3,4},{4,3},{5,6},{6,5},{7,8},{8,7},{9,10},{10,9},{11,... | collective-permute-start | bytes 1179656 | tf_op jit(solution)/shard_map/ppermute | solution.py:386
  31.3 29.6 %all-to-all-start.1 = ((bf16[16,32,128]{2,1,0:T(8,128)(2,1)}), bf16[16,32,128]{2,1,0:T(8,128)(2,1)S(1)}, u32[]{:S(2)}, u32[]{:S(2)}) async-start(bf16[16,32,128]{2,1,0:T(8,128)(2,1)} %broadcast_in_dim.22), calls=%async_computation.1 | async-start | bytes 262144 | tf_op jit(solution)/shard_map/all_to_all | solution.py:390

commit v5 on v4

--- a/solution.py
+++ b/solution.py
@@ -20,6 +20,8 @@
 XY = ("dp_1", "tm_1", "tm_2")
 NEG = -1e30
 ROWS = 32
+HEAD_XY = 23
+HEAD_Z = 10
 SCALE = HD**-0.5
 f32 = jnp.float32
 bf16 = jnp.bfloat16
@@ -369,6 +371,12 @@
     return count
 
 
+def exchange(x, axes, head):
+    count = size_of(axes)
+    groups = [[(i + head) % count for i in range(count)]]
+    return lax.all_to_all(x, axes, 0, 0, axis_index_groups=groups, tiled=True)
+
+
 def step(query_proj, key_proj, value_proj, cotangent, lengths, rel_bias):
     ends = size_of(TM)
     near = [(i, i ^ 1) for i in range(ends)]
@@ -381,13 +389,13 @@
     side_a = lax.ppermute(kv, TM, near)
     s, gp, bias, edge, q2, g2 = own_part(lengths, q, g, table, kv)
     p, ds, p0, ds0, gb = row_part(size_of(XY), lengths, side_a, side_b, s, gp, bias, edge, q2, g2)
-    z = lax.all_to_all(gb, XY, 0, 0, tiled=True)
+    z = exchange(gb, XY, HEAD_XY)
     da, db = side_part(lengths, q, g, p, ds, p0, ds0)
     fb = lax.ppermute(db, TM, far)
     fa = lax.ppermute(da, TM, near)
     z = jnp.sum(z.astype(f32), axis=0).astype(bf16)
     z = jnp.broadcast_to(z[None], (size_of(Z16), ROWS, F))
-    z = lax.all_to_all(z, Z16, 0, 0, tiled=True)
+    z = exchange(z, Z16, HEAD_Z)
     ctx, dq, grad_key, grad_value = output_part(
         lengths, q, g, k, v, stay(side_a), stay(side_b), p, ds, p0, ds0, fa, fb
     )

time: 62.1 us -> 56.8 us (0.915)
  the two profiles are of different devices: /device:TPU:32 before, /device:TPU:7 now
where the time goes in v5:
time: 56.8 us; the launch traced here: 56.4 us
  starting transfers between devices  36.7 us (65%)
  Pallas kernels  10.2 us (18%)
  waiting for transfers between devices  6.6 us (12%)
  between operations  1.39 us (2%)
  local copies, waits for them, and re-layouts  0.78 us (1%)
  other arithmetic  0.69 us (1%)
    all_to_all x2, starting transfers between devices, exchange(): return lax.all_to_all(x, axes, 0, 0, axis_index_groups=groups, tiled=True)  22.8 us
    pallas_call x4, Pallas kernels, in_vmem(): pl.pallas_call(kernel, in_specs=[pl.BlockSpec(memory_space=pltpu.SMEM)] +...  9.16 us
    ppermute x1, starting transfers between devices, step(): fb = lax.ppermute(db, TM, far)  5.62 us
    ppermute x1, starting transfers between devices, step(): side_b = lax.ppermute(kv, TM, far)  4.02 us
    all_to_all x2, waiting for transfers between devices, exchange(): return lax.all_to_all(x, axes, 0, 0, axis_index_groups=groups, tiled=True)  3.87 us
    ppermute x1, waiting for transfers between devices, step(): side_b = lax.ppermute(kv, TM, far)  2.72 us
    ppermute x1, starting transfers between devices, step(): fa = lax.ppermute(da, TM, near)  2.3 us
    ppermute x1, starting transfers between devices, step(): side_a = lax.ppermute(kv, TM, near)  1.92 us
  transfers between devices with their start and end apart: 6, of which 2 were waited for; matrix products, arithmetic and copies ran while one was open for 1% of the time, Pallas kernels for 12%

profile of v5, /device:TPU:7, one launch (start us, length us, event | category | flops | bytes accessed | tf_op | source)
XLA Modules:
  0.0 56.4 jit_solution(12587773617004552594)
XLA Ops:
  0.6 1.0 %stack.1.kv_ref = bf16[2,128,768]{2,1,0:T(8,128)(2,1)S(1)} custom-call(bf16[128,768]{1,0:T(8,128)(2,1)} %bitcast.10, bf16[128,768]{1,0:T(8,128)(2,1)} %bitcast.12), custom_call_target="tpu_custom_call" | custom-call | tf_op jit(solution)/shard_map/stack/pallas_call | solution.py:289
  1.7 4.0 %collective-permute-start.1 = (bf16[2,128,768]{2,1,0:T(8,128)(2,1)S(1)}, bf16[2,128,768]{2,1,0:T(8,128)(2,1)S(1)}, u32[]{:S(2)}, u32[]{:S(2)}) collective-permute-start(bf16[2,128,768]{2,1,0:T(8,128)(2,1)S(1)} %stack.1.kv_ref), channel_id=1, source_target_pairs={{1,2},{2,1},{3,4},{4,3},{5,6},{6,5},{7,8},{8,7},{9,10},{10,9},{11,... | collective-permute-start | bytes 1179656 | tf_op jit(solution)/shard_map/ppermute | solution.py:388
  5.7 1.9 %collective-permute-start = (bf16[2,128,768]{2,1,0:T(8,128)(2,1)S(1)}, bf16[2,128,768]{2,1,0:T(8,128)(2,1)S(1)}, u32[]{:S(2)}, u32[]{:S(2)}) collective-permute-start(bf16[2,128,768]{2,1,0:T(8,128)(2,1)S(1)} %stack.1.kv_ref), channel_id=1, source_target_pairs={{0,1},{1,0},{2,3},{3,2},{4,5},{5,4},{6,7},{7,6},{8,9},{9,8},{10,11... | collective-permute-start | bytes 1179656 | tf_op jit(solution)/shard_map/ppermute | solution.py:389
  8.3 1.9 %shard_map.101 = (f32[6,128,256]{2,1,0:T(8,128)S(1)}, f32[6,128,256]{2,1,0:T(8,128)S(1)}, f32[6,128,256]{2,1,0:T(8,128)S(1)}, f32[6,1,256]{2,1,0:T(1,128)S(1)}, ...) custom-call(s32[1]{0:T(128)S(6)} %copy.13.length_ref, bf16[128,768]{1,0:T(8,128)(2,1)} %bitcast.14, ...), custom_call_target="tpu_custom_call" | custom-call | flops 1073741824 | bytes 4194304 | tf_op jit(solution)/shard_map/pallas_call | solution.py:303
  10.2 2.7 %collective-permute-done.1.b_ref.b_hbm = bf16[2,128,768]{2,1,0:T(8,128)(2,1)S(1)} collective-permute-done((bf16[2,128,768]{2,1,0:T(8,128)(2,1)S(1)}, bf16[2,128,768]{2,1,0:T(8,128)(2,1)S(1)}, u32[]{:S(2)}, u32[]{:S(2)}) %collective-permute-start.1) | collective-permute-done | bytes 393248 | tf_op jit(solution)/shard_map/ppermute | solution.py:388
  12.9 0.0 copy-start
  12.9 0.0 collective-permute-done.a_ref.a_hbm
  12.9 0.0 copy-start.1
  12.9 2.4 %shard_map.102 = (bf16[6,2,128,256]{3,2,1,0:T(8,128)(2,1)S(1)}, bf16[6,2,128,256]{3,2,1,0:T(8,128)(2,1)S(1)}, f32[6,1,256]{2,1,0:T(1,128)S(1)}, f32[6,1,256]{2,1,0:T(1,128)S(1)}, bf16[32,32,128]{2,1,0:T(8,128)(2,1)}) custom-call(s32[1]{0:T(128)S(6)} %copy.13.length_ref, bf16[2,128,768]{2,1,0:T(8,128)(2,1)S(1)} %collective-permute-done.a_ref.a_hbm, ...), custom_call_target="tpu_custom_call" | custom-call | flops 1073741824 | bytes 4194304 | tf_op jit(solution)/shard_map/pallas_call | solution.py:303
  15.3 0.0 copy-done
  15.3 0.0 copy-done.1
  15.3 6.5 %all-to-all-start = ((bf16[32,32,128]{2,1,0:T(8,128)(2,1)}), bf16[32,32,128]{2,1,0:T(8,128)(2,1)S(1)}, u32[]{:S(2)}, u32[]{:S(2)}) async-start(bf16[32,32,128]{2,1,0:T(8,128)(2,1)} %get-tuple-element.38), calls=%async_computation | async-start | bytes 524288 | tf_op jit(solution)/shard_map/all_to_all | solution.py:377
  21.9 1.6 %shard_map.103 = (bf16[2,128,768]{2,1,0:T(8,128)(2,1)S(1)}, bf16[2,128,768]{2,1,0:T(8,128)(2,1)S(1)}) custom-call(s32[1]{0:T(128)S(6)} %copy.13.length_ref, bf16[128,768]{1,0:T(8,128)(2,1)} %bitcast.15, bf16[128,768]{1,0:T(8,128)(2,1)} %bitcast.18, bf16[6,2,128,256]{3,2,1,0:T(8,128)(2,1)S(1)} %get-tuple-element.28.p_ref, ...), custom_call_target="tpu_custom_call" | custom-call | flops 1073741824 | bytes 4194304 | tf_op jit(solution)/shard_map/pallas_call | solution.py:303
  23.5 2.3 %collective-permute-start.2 = (bf16[2,128,768]{2,1,0:T(8,128)(2,1)S(1)}, bf16[2,128,768]{2,1,0:T(8,128)(2,1)S(1)}, u32[]{:S(2)}, u32[]{:S(2)}) collective-permute-start(bf16[2,128,768]{2,1,0:T(8,128)(2,1)S(1)} %get-tuple-element.32), channel_id=1, source_target_pairs={{0,1},{1,0},{2,3},{3,2},{4,5},{5,4},{6,7},{7,6},{8,9},{9,8},{10,11... | collective-permute-start | bytes 1179656 | tf_op jit(solution)/shard_map/ppermute | solution.py:395
  25.8 5.6 %collective-permute-start.3 = (bf16[2,128,768]{2,1,0:T(8,128)(2,1)S(1)}, bf16[2,128,768]{2,1,0:T(8,128)(2,1)S(1)}, u32[]{:S(2)}, u32[]{:S(2)}) collective-permute-start(bf16[2,128,768]{2,1,0:T(8,128)(2,1)S(1)} %get-tuple-element.33), channel_id=1, source_target_pairs={{1,2},{2,1},{3,4},{4,3},{5,6},{6,5},{7,8},{8,7},{9,10},{10,9},{11,... | collective-permute-start | bytes 1179656 | tf_op jit(solution)/shard_map/ppermute | solution.py:394
  31.5 0.0 all-to-all-done
  31.5 0.1 reduce_sum.21
  31.5 0.7 %broadcast_in_dim.22 = bf16[16,32,128]{2,1,0:T(8,128)(2,1)} broadcast(bf16[32,128]{1,0:T(8,128)(2,1)S(1)} %reduce_sum.21), dimensions={1,2} | broadcast | bytes 139264 | tf_op jit(solution)/shard_map/broadcast_in_dim | solution.py:397
  32.2 16.3 %all-to-all-start.1 = ((bf16[16,32,128]{2,1,0:T(8,128)(2,1)}), bf16[16,32,128]{2,1,0:T(8,128)(2,1)S(1)}, u32[]{:S(2)}, u32[]{:S(2)}) async-start(bf16[16,32,128]{2,1,0:T(8,128)(2,1)} %broadcast_in_dim.22), calls=%async_computation.1 | async-start | bytes 262144 | tf_op jit(solution)/shard_map/all_to_all | solution.py:377
  48.5 0.0 collective-permute-done.2.fa_ref
  48.5 0.0 collective-permute-done.3.fb_ref
  48.5 3.2 %shard_map.104 = (bf16[128,768]{1,0:T(8,128)(2,1)}, bf16[128,768]{1,0:T(8,128)(2,1)}, bf16[128,768]{1,0:T(8,128)(2,1)}, bf16[128,768]{1,0:T(8,128)(2,1)}) custom-call(s32[1]{0:T(128)S(6)} %copy.13.length_ref, bf16[128,768]{1,0:T(8,128)(2,1)} %bitcast.16, bf16[128,768]{1,0:T(8,128)(2,1)} %bitcast.19, bf16[128,768]{1,0:T(8,128)(2,1)} %bitcast.11, ...), custom_call_target="tpu_custom_call" | custom-call | flops 1073741824 | bytes 4194304 | tf_op jit(solution)/shard_map/pallas_call | solution.py:303
  51.7 3.9 %all-to-all-done.1 = bf16[16,32,128]{2,1,0:T(8,128)(2,1)S(1)} async-done(((bf16[16,32,128]{2,1,0:T(8,128)(2,1)}), bf16[16,32,128]{2,1,0:T(8,128)(2,1)S(1)}, u32[]{:S(2)}, u32[]{:S(2)}) %all-to-all-start.1) | async-done | bytes 131104 | tf_op jit(solution)/shard_map/all_to_all | solution.py:377
  55.6 0.1 copy.12
  55.7 0.6 %pad_maximum_fusion = f32[12,257]{1,0:T(8,128)} fusion(f32[12,1]{1,0:T(8,128)S(1)} %copy.12, f32[12,128]{1,0:T(8,128)S(1)} %get-tuple-element.40, f32[12,128]{1,0:T(8,128)S(1)} %get-tuple-element.39), kind=kLoop, calls=%fused_computation.1 | loop fusion | flops 6168 | bytes 24672 | tf_op jit(solution)/shard_map/concatenate | solution.py:403
  (3 shorter events, 0.0 us)
Async XLA Ops:
  1.7 11.2 %collective-permute-start.1 = (bf16[2,128,768]{2,1,0:T(8,128)(2,1)S(1)}, bf16[2,128,768]{2,1,0:T(8,128)(2,1)S(1)}, u32[]{:S(2)}, u32[]{:S(2)}) collective-permute-start(bf16[2,128,768]{2,1,0:T(8,128)(2,1)S(1)} %stack.1.kv_ref), channel_id=1, source_target_pairs={{1,2},{2,1},{3,4},{4,3},{5,6},{6,5},{7,8},{8,7},{9,10},{10,9},{11,... | collective-permute-start | bytes 1179656 | tf_op jit(solution)/shard_map/ppermute | solution.py:388
  5.7 7.2 %collective-permute-start = (bf16[2,128,768]{2,1,0:T(8,128)(2,1)S(1)}, bf16[2,128,768]{2,1,0:T(8,128)(2,1)S(1)}, u32[]{:S(2)}, u32[]{:S(2)}) collective-permute-start(bf16[2,128,768]{2,1,0:T(8,128)(2,1)S(1)} %stack.1.kv_ref), channel_id=1, source_target_pairs={{0,1},{1,0},{2,3},{3,2},{4,5},{5,4},{6,7},{7,6},{8,9},{9,8},{10,11... | collective-permute-start | bytes 1179656 | tf_op jit(solution)/shard_map/ppermute | solution.py:389
  12.9 2.4 %copy-start = (bf16[2,128,768]{2,1,0:T(8,128)(2,1)}, bf16[2,128,768]{2,1,0:T(8,128)(2,1)S(1)}, u32[]{:S(2)}) copy-start(bf16[2,128,768]{2,1,0:T(8,128)(2,1)S(1)} %collective-permute-done.1.b_ref.b_hbm) | copy-start | bytes 1179652
  12.9 2.4 %copy-start.1 = (bf16[2,128,768]{2,1,0:T(8,128)(2,1)}, bf16[2,128,768]{2,1,0:T(8,128)(2,1)S(1)}, u32[]{:S(2)}) copy-start(bf16[2,128,768]{2,1,0:T(8,128)(2,1)S(1)} %collective-permute-done.a_ref.a_hbm) | copy-start | bytes 1179652
  15.3 16.1 %all-to-all-start = ((bf16[32,32,128]{2,1,0:T(8,128)(2,1)}), bf16[32,32,128]{2,1,0:T(8,128)(2,1)S(1)}, u32[]{:S(2)}, u32[]{:S(2)}) async-start(bf16[32,32,128]{2,1,0:T(8,128)(2,1)} %get-tuple-element.38), calls=%async_computation | async-start | bytes 524288 | tf_op jit(solution)/shard_map/all_to_all | solution.py:377
  23.5 25.0 %collective-permute-start.2 = (bf16[2,128,768]{2,1,0:T(8,128)(2,1)S(1)}, bf16[2,128,768]{2,1,0:T(8,128)(2,1)S(1)}, u32[]{:S(2)}, u32[]{:S(2)}) collective-permute-start(bf16[2,128,768]{2,1,0:T(8,128)(2,1)S(1)} %get-tuple-element.32), channel_id=1, source_target_pairs={{0,1},{1,0},{2,3},{3,2},{4,5},{5,4},{6,7},{7,6},{8,9},{9,8},{10,11... | collective-permute-start | bytes 1179656 | tf_op jit(solution)/shard_map/ppermute | solution.py:395
  25.8 22.7 %collective-permute-start.3 = (bf16[2,128,768]{2,1,0:T(8,128)(2,1)S(1)}, bf16[2,128,768]{2,1,0:T(8,128)(2,1)S(1)}, u32[]{:S(2)}, u32[]{:S(2)}) collective-permute-start(bf16[2,128,768]{2,1,0:T(8,128)(2,1)S(1)} %get-tuple-element.33), channel_id=1, source_target_pairs={{1,2},{2,1},{3,4},{4,3},{5,6},{6,5},{7,8},{8,7},{9,10},{10,9},{11,... | collective-permute-start | bytes 1179656 | tf_op jit(solution)/shard_map/ppermute | solution.py:394
  32.2 23.4 %all-to-all-start.1 = ((bf16[16,32,128]{2,1,0:T(8,128)(2,1)}), bf16[16,32,128]{2,1,0:T(8,128)(2,1)S(1)}, u32[]{:S(2)}, u32[]{:S(2)}) async-start(bf16[16,32,128]{2,1,0:T(8,128)(2,1)} %broadcast_in_dim.22), calls=%async_computation.1 | async-start | bytes 262144 | tf_op jit(solution)/shard_map/all_to_all | solution.py:377
